TPU v7x, 32 devices: a whole 2x2x4 slice. The times are simulated.
32 devices in a mesh: shard: 4 (over z), ctx: 4 (over y, x), tp: 2 (over core).
Axes of the slice: x: 2, y: 2, z: 4, core: 2. Of those that a mesh axis runs over, the one named last changes fastest.
Arguments:
- tokens: bfloat16 [32, 1024, 768], P('shard', ('ctx', 'tp')), may hold values from -6 to 6
- project_weight: bfloat16 [768, 3, 768], P(('shard', 'ctx'), None, 'tp'), may hold values from -0.21875 to 0.21875
- attend_weight: bfloat16 [768, 768], P('tp', ('shard', 'ctx')), may hold values from -1.25 to 1.25
- up_weight: bfloat16 [768, 3072], P(('shard', 'ctx'), 'tp'), may hold values from -0.21875 to 0.21875
- down_weight: bfloat16 [3072, 768], P('tp', ('shard', 'ctx')), may hold values from -0.109375 to 0.109375
- project_bias: bfloat16 [3, 768], P(None, ('shard', 'ctx')), may hold values from -3 to 3
- attend_bias: bfloat16 [768], P(('shard', 'ctx')), may hold values from -3 to 3
- up_bias: bfloat16 [3072], P(('shard', 'ctx')), may hold values from -3 to 3
- down_bias: bfloat16 [768], P(('shard', 'ctx')), may hold values from -3 to 3
- first_gain: bfloat16 [768], P(('shard', 'ctx')), may hold values from 0.25 to 1.75
- first_shift: bfloat16 [768], P(('shard', 'ctx')), may hold values from -2 to 2
- second_gain: bfloat16 [768], P(('shard', 'ctx')), may hold values from 0.25 to 1.75
- second_shift: bfloat16 [768], P(('shard', 'ctx')), may hold values from -2 to 2
- segment_ids: int32 [32, 1024], P('shard'), may hold values from 0 to 63, never falling along the last dimension, each value on 1 to 512 neighbouring positions
- padding: int32 [32, 1024], P('shard'), may hold values 0 or 1
- cotangent: bfloat16 [32, 1024, 768], P('shard', ('ctx', 'tp')), may hold values from -6 to 6
Outputs:
- output: bfloat16 [32, 1024, 768], P('shard', ('ctx', 'tp'))
- tokens_grad: bfloat16 [32, 1024, 768], P('shard', ('ctx', 'tp'))
- project_weight_grad: float32 [768, 3, 768], P(('shard', 'ctx'), None, 'tp')
- attend_weight_grad: float32 [768, 768], P('tp', ('shard', 'ctx'))
- up_weight_grad: float32 [768, 3072], P(('shard', 'ctx'), 'tp')
- down_weight_grad: float32 [3072, 768], P('tp', ('shard', 'ctx'))
- project_bias_grad: float32 [3, 768], P(None, ('shard', 'ctx'))
- attend_bias_grad: float32 [768], P(('shard', 'ctx'))
- up_bias_grad: float32 [3072], P(('shard', 'ctx'))
- down_bias_grad: float32 [768], P(('shard', 'ctx'))
- first_gain_grad: float32 [768], P(('shard', 'ctx'))
- first_shift_grad: float32 [768], P(('shard', 'ctx'))
- second_gain_grad: float32 [768], P(('shard', 'ctx'))
- second_shift_grad: float32 [768], P(('shard', 'ctx'))
Inputs may be any that keep to these rules, and one draw needn't show every extreme that they name: `segment_ids`: segment numbers never fall along a sequence; a segment has 1 to 512 positions, and some segment of the draw has exactly 512.
All inputs are finite; a program needn't handle non-finite values. No bound on the sum of `padding` on one device may be relied on, other than what follows from the above.
Results may differ from a plain program's by a relative error of at most 0.02.
Values may be sent and summed in bfloat16 or wider, within the bound.
A program may use at most 320 MiB of HBM per device.

v0:
```python
import math

import jax
import jax.numpy as jnp
from jax import lax
from jax.sharding import PartitionSpec as P

D = 768
HEADS = 12
HEAD_DIM = 64
FF = 3072
S = 1024


norm_eps = 1e-12
mask_fill = -1000000000.0


def angles(first, count, width):
    position = (first + jnp.arange(count, dtype=jnp.int32)).astype(jnp.float32)
    column = jnp.arange(width, dtype=jnp.int32) % HEAD_DIM // 2
    rate = jnp.exp(column.astype(jnp.float32) * (-2.0 * math.log(10000.0) / HEAD_DIM))
    phase = position[:, None] * rate[None, :]
    return (jnp.cos(phase), jnp.sin(phase))


def rotate(values, cosine, sine):
    even = jnp.arange(values.shape[-1], dtype=jnp.int32) % 2 == 0
    partner = jnp.where(even, -jnp.roll(values, -1, axis=-1), jnp.roll(values, 1, axis=-1))
    return values * cosine + partner * sine


def normalize(rows, gain, shift):
    mean = jnp.mean(rows, axis=-1, keepdims=True)
    centred = rows - mean
    factor = lax.rsqrt(jnp.mean(centred * centred, axis=-1, keepdims=True) + norm_eps)
    unit = centred * factor
    return (unit * gain + shift, unit, factor)


def normalize_back(incoming, unit, factor, gain):
    gain_grad = jnp.sum(incoming * unit, axis=(0, 1))
    shift_grad = jnp.sum(incoming, axis=(0, 1))
    inner = incoming * gain
    rows_grad = factor * (
        inner
        - jnp.mean(inner, axis=-1, keepdims=True)
        - unit * jnp.mean(inner * unit, axis=-1, keepdims=True)
    )
    return (rows_grad, gain_grad, shift_grad)


def gelu_slope(values):
    cumulative = 0.5 * (1.0 + lax.erf(values * (1.0 / math.sqrt(2.0))))
    density = jnp.exp(-0.5 * values * values) * (1.0 / math.sqrt(2.0 * math.pi))
    return cumulative + values * density


def split_heads(array, heads):
    return array.reshape(array.shape[:2] + (heads, array.shape[2] // heads))


def merge_heads(array):
    return array.reshape(array.shape[:2] + (array.shape[2] * array.shape[3],))


def head_scores(queries, keyset, allowed, heads):
    raw = jnp.einsum(
        "gqhd,gkhd->ghqk",
        split_heads(queries, heads),
        split_heads(keyset, heads),
        preferred_element_type=jnp.float32,
    )
    return jnp.where(allowed[:, None], raw * (1.0 / math.sqrt(HEAD_DIM)), mask_fill)


def attend(queries, keyset, valueset, allowed, heads):
    scores = head_scores(queries, keyset, allowed, heads)
    top = jnp.max(scores, axis=-1, keepdims=True)
    expo = jnp.exp(scores - top)
    total = jnp.sum(expo, axis=-1, keepdims=True)
    probs = (expo / total).astype(jnp.bfloat16)
    mixed = jnp.einsum(
        "ghqk,gkhd->gqhd", probs, split_heads(valueset, heads), preferred_element_type=jnp.float32
    )
    return (merge_heads(mixed), top, total)


def softmax_grad(queries, keyset, valueset, allowed, top, total, out_grads, heads):
    scores = head_scores(queries, keyset, allowed, heads)
    probs = jnp.exp(scores - top) / total
    prob_grad = jnp.einsum(
        "gqhd,gkhd->ghqk",
        split_heads(out_grads, heads),
        split_heads(valueset, heads),
        preferred_element_type=jnp.float32,
    )
    return (probs, prob_grad)


def attend_back(queries, keyset, valueset, allowed, top, total, out_grads, heads):
    probs, prob_grad = softmax_grad(
        queries, keyset, valueset, allowed, top, total, out_grads, heads
    )
    inner = jnp.sum(probs * prob_grad, axis=-1, keepdims=True)
    score_grad = (probs * (prob_grad - inner)).astype(jnp.bfloat16)
    scale = 1.0 / math.sqrt(HEAD_DIM)
    query_grad = (
        jnp.einsum(
            "ghqk,gkhd->gqhd",
            score_grad,
            split_heads(keyset, heads),
            preferred_element_type=jnp.float32,
        )
        * scale
    )
    key_grad = (
        jnp.einsum(
            "ghqk,gqhd->gkhd",
            score_grad,
            split_heads(queries, heads),
            preferred_element_type=jnp.float32,
        )
        * scale
    )
    value_grad = jnp.einsum(
        "ghqk,gqhd->gkhd",
        probs.astype(jnp.bfloat16),
        split_heads(out_grads, heads),
        preferred_element_type=jnp.float32,
    )
    return (merge_heads(query_grad), merge_heads(key_grad), merge_heads(value_grad))


def contract_rows(left, right):
    return lax.dot_general(
        left, right, (((0,), (0,)), ((), ())), preferred_element_type=jnp.float32
    )


def contract_cols(left, right):
    return lax.dot_general(
        left, right, (((1,), (1,)), ((), ())), preferred_element_type=jnp.float32
    )


def copies(vector, count):
    return jnp.broadcast_to(vector[None], (count,) + vector.shape)


def local(
    tokens,
    project_weight,
    attend_weight,
    up_weight,
    down_weight,
    project_bias,
    attend_bias,
    up_bias,
    down_bias,
    first_gain,
    first_shift,
    second_gain,
    second_shift,
    segment_ids,
    padding,
    cotangent,
):
    tensor_count = lax.axis_size("tp")
    tensor_index = lax.axis_index("tp")
    context_index = lax.axis_index("ctx")
    local_width = D // tensor_count
    local_hidden = FF // tensor_count
    local_heads = HEADS // tensor_count
    block_rows = S // lax.axis_size("ctx")
    seq_count = tokens.shape[0]
    row_total = seq_count * block_rows
    group = math.gcd(seq_count, 4)

    def grouped(array):
        return array.reshape((seq_count // group, group) + array.shape[1:])

    def ungroup(array):
        return array.reshape((seq_count,) + array.shape[2:])

    (
        project_full,
        attend_full,
        up_full,
        down_full,
        project_shift,
        attend_shift,
        up_shift,
        down_shift,
        gain_one,
        shift_one,
        gain_two,
        shift_two,
    ) = (
        lax.all_gather(project_weight, ("shard", "ctx"), axis=0, tiled=True),
        lax.all_gather(attend_weight, ("shard", "ctx"), axis=1, tiled=True),
        lax.all_gather(up_weight, ("shard", "ctx"), axis=0, tiled=True),
        lax.all_gather(down_weight, ("shard", "ctx"), axis=1, tiled=True),
        lax.all_gather(project_bias, ("shard", "ctx"), axis=1, tiled=True),
        lax.all_gather(attend_bias, ("shard", "ctx"), axis=0, tiled=True),
        lax.all_gather(up_bias, ("shard", "ctx"), axis=0, tiled=True),
        lax.all_gather(down_bias, ("shard", "ctx"), axis=0, tiled=True),
        lax.all_gather(first_gain, ("shard", "ctx"), axis=0, tiled=True),
        lax.all_gather(first_shift, ("shard", "ctx"), axis=0, tiled=True),
        lax.all_gather(second_gain, ("shard", "ctx"), axis=0, tiled=True),
        lax.all_gather(second_shift, ("shard", "ctx"), axis=0, tiled=True),
    )
    project_matrix = project_full.reshape(D, 3 * local_width)
    project_local = (
        lax.dynamic_slice_in_dim(project_shift, tensor_index * local_width, local_width, 1)
        .astype(jnp.float32)
        .reshape(3 * local_width)
    )
    up_local = lax.dynamic_slice_in_dim(
        up_shift, tensor_index * local_hidden, local_hidden, 0
    ).astype(jnp.float32)
    attend_shift = attend_shift.astype(jnp.float32)
    down_shift = down_shift.astype(jnp.float32)
    gain_one = gain_one.astype(jnp.float32)
    shift_one = shift_one.astype(jnp.float32)
    gain_two = gain_two.astype(jnp.float32)
    shift_two = shift_two.astype(jnp.float32)
    own_segments = lax.dynamic_slice_in_dim(segment_ids, context_index * block_rows, block_rows, 1)
    own_padding = lax.dynamic_slice_in_dim(padding, context_index * block_rows, block_rows, 1)
    allowed = (own_segments[:, :, None] == segment_ids[:, None, :]) & (
        padding[:, None, :] >= own_padding[:, :, None]
    )
    block_tokens = lax.all_gather(tokens, "tp", axis=1, tiled=True)
    flat_tokens = block_tokens.reshape(row_total, D)
    joint = (
        jnp.dot(flat_tokens, project_matrix, preferred_element_type=jnp.float32)
        + project_local[None]
    )
    joint = joint.reshape(seq_count, block_rows, 3 * local_width)
    cosine, sine = angles(context_index * block_rows, block_rows, local_width)
    query_rot = rotate(joint[..., :local_width], cosine, sine).astype(jnp.bfloat16)
    key_rot = rotate(joint[..., local_width : 2 * local_width], cosine, sine).astype(jnp.bfloat16)
    value_low = joint[..., 2 * local_width :].astype(jnp.bfloat16)
    all_keys, all_values = (
        lax.all_gather(key_rot, "ctx", axis=1, tiled=True),
        lax.all_gather(value_low, "ctx", axis=1, tiled=True),
    )

    def forward_group(items):
        return attend(items[0], items[1], items[2], items[3], local_heads)

    attended, top, total = lax.map(
        forward_group,
        (grouped(query_rot), grouped(all_keys), grouped(all_values), grouped(allowed)),
    )
    attended_flat = ungroup(attended).astype(jnp.bfloat16).reshape(row_total, local_width)
    attend_part = jnp.dot(attended_flat, attend_full, preferred_element_type=jnp.float32).reshape(
        seq_count, block_rows, D
    )
    branch = (
        lax.psum_scatter(
            attend_part.astype(jnp.bfloat16), "tp", scatter_dimension=1, tiled=True
        ).astype(jnp.float32)
        + attend_shift
    )
    first_out, first_unit, first_factor = normalize(
        tokens.astype(jnp.float32) + branch, gain_one, shift_one
    )
    first_rows = lax.all_gather(first_out.astype(jnp.bfloat16), "tp", axis=1, tiled=True).reshape(
        row_total, D
    )
    pre = jnp.dot(first_rows, up_full, preferred_element_type=jnp.float32) + up_local[None]
    hidden = jax.nn.gelu(pre, approximate=False).astype(jnp.bfloat16)
    down_part = jnp.dot(hidden, down_full, preferred_element_type=jnp.float32).reshape(
        seq_count, block_rows, D
    )
    ffn = (
        lax.psum_scatter(
            down_part.astype(jnp.bfloat16), "tp", scatter_dimension=1, tiled=True
        ).astype(jnp.float32)
        + down_shift
    )
    second_out, second_unit, second_factor = normalize(first_out + ffn, gain_two, shift_two)
    output = second_out.astype(jnp.bfloat16)
    second_grad, second_gain_grad, second_shift_grad = normalize_back(
        cotangent.astype(jnp.float32), second_unit, second_factor, gain_two
    )
    ffn_low = second_grad.astype(jnp.bfloat16)
    down_bias_grad = jnp.sum(ffn_low.astype(jnp.float32), axis=(0, 1))
    ffn_rows = lax.all_gather(ffn_low, "tp", axis=1, tiled=True).reshape(row_total, D)
    down_weight_grad = contract_rows(hidden, ffn_rows)
    pre_grad = (contract_cols(ffn_rows, down_full) * gelu_slope(pre)).astype(jnp.bfloat16)
    up_bias_local = jnp.sum(pre_grad.astype(jnp.float32), axis=0)
    up_weight_grad = contract_rows(first_rows, pre_grad)
    first_part = contract_cols(pre_grad, up_full).reshape(seq_count, block_rows, D)
    first_total = second_grad + lax.psum_scatter(
        first_part.astype(jnp.bfloat16), "tp", scatter_dimension=1, tiled=True
    ).astype(jnp.float32)
    first_grad, first_gain_grad, first_shift_grad = normalize_back(
        first_total, first_unit, first_factor, gain_one
    )
    branch_low = first_grad.astype(jnp.bfloat16)
    attend_bias_grad = jnp.sum(branch_low.astype(jnp.float32), axis=(0, 1))
    branch_rows = lax.all_gather(branch_low, "tp", axis=1, tiled=True).reshape(row_total, D)
    attend_weight_grad = contract_rows(attended_flat, branch_rows)
    attended_grad = (
        contract_cols(branch_rows, attend_full)
        .astype(jnp.bfloat16)
        .reshape(seq_count, block_rows, local_width)
    )

    def back_group(items):
        return attend_back(
            items[0], items[1], items[2], items[3], items[4], items[5], items[6], local_heads
        )

    query_part, key_part, value_part = lax.map(
        back_group,
        (
            grouped(query_rot),
            grouped(all_keys),
            grouped(all_values),
            grouped(allowed),
            top,
            total,
            grouped(attended_grad),
        ),
    )
    key_rot_grad, value_grad = (
        lax.psum_scatter(
            ungroup(key_part).astype(jnp.bfloat16), "ctx", scatter_dimension=1, tiled=True
        ).astype(jnp.float32),
        lax.psum_scatter(
            ungroup(value_part).astype(jnp.bfloat16), "ctx", scatter_dimension=1, tiled=True
        ).astype(jnp.float32),
    )
    query_rot_grad = ungroup(query_part)
    query_grad = rotate(query_rot_grad, cosine, -sine)
    key_grad = rotate(key_rot_grad, cosine, -sine)
    joint_grad = (
        jnp.concatenate([query_grad, key_grad, value_grad], axis=-1)
        .astype(jnp.bfloat16)
        .reshape(row_total, 3 * local_width)
    )
    project_bias_local = jnp.sum(joint_grad.astype(jnp.float32), axis=0).reshape(3, local_width)
    project_weight_grad = contract_rows(flat_tokens, joint_grad).reshape(D, 3, local_width)
    token_part = contract_cols(joint_grad, project_matrix).reshape(seq_count, block_rows, D)
    project_bias_full = lax.dynamic_update_slice(
        jnp.zeros((3, D), jnp.float32), project_bias_local, (0, tensor_index * local_width)
    )
    up_bias_full = lax.dynamic_update_slice(
        jnp.zeros((FF,), jnp.float32), up_bias_local, (tensor_index * local_hidden,)
    )
    summed = (
        lax.psum_scatter(
            token_part.astype(jnp.bfloat16), "tp", scatter_dimension=1, tiled=True
        ).astype(jnp.float32),
        lax.psum_scatter(
            copies(project_bias_full, tensor_count).astype(jnp.bfloat16),
            "tp",
            scatter_dimension=0,
            tiled=True,
        ).astype(jnp.float32),
        lax.psum_scatter(
            copies(attend_bias_grad, tensor_count).astype(jnp.bfloat16),
            "tp",
            scatter_dimension=0,
            tiled=True,
        ).astype(jnp.float32),
        lax.psum_scatter(
            copies(up_bias_full, tensor_count).astype(jnp.bfloat16),
            "tp",
            scatter_dimension=0,
            tiled=True,
        ).astype(jnp.float32),
        lax.psum_scatter(
            copies(down_bias_grad, tensor_count).astype(jnp.bfloat16),
            "tp",
            scatter_dimension=0,
            tiled=True,
        ).astype(jnp.float32),
        lax.psum_scatter(
            copies(first_gain_grad, tensor_count).astype(jnp.bfloat16),
            "tp",
            scatter_dimension=0,
            tiled=True,
        ).astype(jnp.float32),
        lax.psum_scatter(
            copies(first_shift_grad, tensor_count).astype(jnp.bfloat16),
            "tp",
            scatter_dimension=0,
            tiled=True,
        ).astype(jnp.float32),
        lax.psum_scatter(
            copies(second_gain_grad, tensor_count).astype(jnp.bfloat16),
            "tp",
            scatter_dimension=0,
            tiled=True,
        ).astype(jnp.float32),
        lax.psum_scatter(
            copies(second_shift_grad, tensor_count).astype(jnp.bfloat16),
            "tp",
            scatter_dimension=0,
            tiled=True,
        ).astype(jnp.float32),
    )
    tokens_grad = (first_grad + summed[0]).astype(jnp.bfloat16)
    reduced = (
        lax.psum_scatter(project_weight_grad, ("shard", "ctx"), scatter_dimension=0, tiled=True),
        lax.psum_scatter(attend_weight_grad, ("shard", "ctx"), scatter_dimension=1, tiled=True),
        lax.psum_scatter(up_weight_grad, ("shard", "ctx"), scatter_dimension=0, tiled=True),
        lax.psum_scatter(down_weight_grad, ("shard", "ctx"), scatter_dimension=1, tiled=True),
        lax.psum_scatter(summed[1][0], ("shard", "ctx"), scatter_dimension=1, tiled=True),
        lax.psum_scatter(summed[2][0], ("shard", "ctx"), scatter_dimension=0, tiled=True),
        lax.psum_scatter(summed[3][0], ("shard", "ctx"), scatter_dimension=0, tiled=True),
        lax.psum_scatter(summed[4][0], ("shard", "ctx"), scatter_dimension=0, tiled=True),
        lax.psum_scatter(summed[5][0], ("shard", "ctx"), scatter_dimension=0, tiled=True),
        lax.psum_scatter(summed[6][0], ("shard", "ctx"), scatter_dimension=0, tiled=True),
        lax.psum_scatter(summed[7][0], ("shard", "ctx"), scatter_dimension=0, tiled=True),
        lax.psum_scatter(summed[8][0], ("shard", "ctx"), scatter_dimension=0, tiled=True),
    )
    return (
        output,
        tokens_grad,
        reduced[0],
        reduced[1],
        reduced[2],
        reduced[3],
        reduced[4],
        reduced[5],
        reduced[6],
        reduced[7],
        reduced[8],
        reduced[9],
        reduced[10],
        reduced[11],
    )


def solution(mesh):
    in_specs = (
        P("shard", ("ctx", "tp"), None),
        P(("shard", "ctx"), None, "tp"),
        P("tp", ("shard", "ctx")),
        P(("shard", "ctx"), "tp"),
        P("tp", ("shard", "ctx")),
        P(None, ("shard", "ctx")),
        P(("shard", "ctx")),
        P(("shard", "ctx")),
        P(("shard", "ctx")),
        P(("shard", "ctx")),
        P(("shard", "ctx")),
        P(("shard", "ctx")),
        P(("shard", "ctx")),
        P("shard", None),
        P("shard", None),
        P("shard", ("ctx", "tp"), None),
    )
    out_specs = (
        P("shard", ("ctx", "tp"), None),
        P("shard", ("ctx", "tp"), None),
        P(("shard", "ctx"), None, "tp"),
        P("tp", ("shard", "ctx")),
        P(("shard", "ctx"), "tp"),
        P("tp", ("shard", "ctx")),
        P(None, ("shard", "ctx")),
        P(("shard", "ctx")),
        P(("shard", "ctx")),
        P(("shard", "ctx")),
        P(("shard", "ctx")),
        P(("shard", "ctx")),
        P(("shard", "ctx")),
        P(("shard", "ctx")),
    )
    return jax.shard_map(local, mesh=mesh, in_specs=in_specs, out_specs=out_specs, check_vma=False)
```

profile of v0, /device:TPU:0, one launch (start us, length us, event | category | flops | bytes accessed | tf_op | source)
XLA Modules:
  0.0 1663.8 jit_solution(4468037681128971400)
XLA Ops:
  8.7 42.7 %all-gather = bf16[16,48,3]{1,2,0:T(4,128)(2,1)S(1)} all-gather(bf16[1,48,3]{1,2,0:T(4,128)(2,1)} %bitcast.218), channel_id=1, replica_groups=mesh['shard'=4,'ctx'=4,'tp'=2] {'shard','ctx'}, dimensions={0}, use_global_device_ids=true | all-gather | bytes 4896 | tf_op jit(solution)/shard_map/all_gather | solution.py:204
  51.6 20.8 %all-gather.13.cloned.1.call-done = bf16[768,3,384]{2,0,1:T(8,128)(2,1)} async-done(((bf16[48,3,384]{2,0,1:T(8,128)(2,1)}), bf16[768,3,384]{2,0,1:T(8,128)(2,1)}) %all-gather.13.cloned.1.call-update) | async-done | bytes 1769488 | tf_op jit(solution)/shard_map/all_gather | solution.py:200
  128.1 48.8 %all_gather.59 = bf16[384,768]{0,1:T(8,128)(2,1)} all-gather(bf16[384,48]{0,1:T(8,128)(2,1)} %param.22), channel_id=1, replica_groups=mesh['shard'=4,'ctx'=4,'tp'=2] {'shard','ctx'}, dimensions={1}, use_global_device_ids=true | all-gather | bytes 626688 | tf_op jit(solution)/shard_map/all_gather | solution.py:201
  190.7 60.3 %all-gather.17.cloned.1.call-done = bf16[8,1024,384]{2,1,0:T(8,128)(2,1)} async-done(((bf16[8,256,384]{2,1,0:T(8,128)(2,1)}), bf16[8,1024,384]{2,1,0:T(8,128)(2,1)}) %all-gather.17.cloned.1.call-update) | async-done | bytes 6291472 | tf_op jit(solution)/shard_map/all_gather | solution.py:245
  259.7 84.1 %while.28 = (s32[]{:T(128)}, bf16[2,4,256,384]{2,3,1,0:T(8,128)(2,1)}, f32[2,4,6,256,1]{3,2,1,4,0:T(8,128)S(1)}, f32[2,4,6,256,1]{3,2,1,4,0:T(8,128)S(1)}, bf16[...) while((s32[]{:T(128)}, ...), condition=%wide.region_3.4_spmd, body=%wide.region_0.3_spmd.sunk | while | flops 1686097920 | bytes 129753232 | solution.py:252
  354.4 76.6 %all-reduce.23 = (bf16[768]{0:T(1024)(128)(2,1)S(1)}, bf16[768]{0:T(1024)(128)(2,1)S(1)}, bf16[768]{0:T(1024)(128)(2,1)S(1)}, bf16[3072]{0:T(1024)(128)(2,1)S(1)...) all-reduce(bf16[768]{0:T(1024)(128)(2,1)S(1)} %dynamic-update-slice, ...), channel_id=1, replica_groups=mesh['shard'=4,'ctx'=4,'tp'=2] {'shard','ctx'}, use_global_device_ids=true, to_apply=%add.2 | all-reduce | flops 7680 | bytes 30720
  444.3 34.6 %fusion.9 = (bf16[2048,1536]{1,0:T(8,128)(2,1)}, f32[2048,1536]{1,0:T(8,128)}) fusion(f32[1536]{0:T(1024)S(1)} %dynamic-slice_convert_fusion.1, bf16[2048,768]{1,0:T(8,128)(2,1)} %bitcast.220, bf16[768,1536]{1,0:T(8,128)(2,1)} %all-gather.21.cloned.1.call-done), kind=kOutput, calls=%fused_computation.36 | convolution fusion | flops 5039456256 | bytes 24385536 | tf_op jit(solution)/shard_map/dot_general | solution.py:272
  478.8 32.1 %all-gather.23.cloned.1.call-done = bf16[1536,768]{0,1:T(8,128)(2,1)} async-done(((bf16[1536,48]{0,1:T(8,128)(2,1)}), bf16[1536,768]{0,1:T(8,128)(2,1)}) %all-gather.23.cloned.1.call-update) | async-done | bytes 2359312 | tf_op jit(solution)/shard_map/all_gather | solution.py:203
  539.9 13.4 all-gather.25.cloned.1.call-done
  553.3 12.4 convert_reduce_fusion
  572.2 12.2 reduce-scatter.18.cloned.1.call-done
  594.1 13.3 all-gather.27.cloned.1.call-done
  611.3 195.9 %while.29 = (s32[]{:T(128)}, f32[2,4,256,384]{3,2,1,0:T(8,128)}, bf16[2,4,1024,384]{2,3,1,0:T(8,128)(2,1)}, bf16[2,4,1024,384]{2,3,1,0:T(8,128)(2,1)}, bf16[2,4,...) while((s32[]{:T(128)}, f32[2,4,256,384]{3,2,1,0:T(8,128)}, ...), condition=%wide.region_17.18_spmd, body=%wide.region_15.17_spmd.sunk | while | flops 4092979200 | bytes 280166688 | solution.py:317
  628.5 20.0 %multiply_reduce_fusion.7 = (f32[4,6,256]{2,1,0:T(8,128)S(1)}, f32[4,6,256,1024]{3,2,1,0:T(8,128)}) fusion(f32[4,6,256,1024]{3,2,1,0:T(8,128)} %fusion.160, f32[4,6,256]{2,1,0:T(8,128)S(1)} %get-tuple-element.429, f32[4,6,256]{2,1,0:T(8,128)S(1)} %get-tuple-element.430, bf16[4,256,6,64]{1,3,2,0:T(8,128)(2,1)S(1)} %bitcast.187, ...), kind=kOutput, calls=%fused_computation.16.clone.1 | convolution fusion | flops 843048960 | bytes 55386112 | tf_op jit(solution)/shard_map/while/body/eval_jaxpr/gqhd,gkhd->ghqk/dot_general | solution.py:68
  648.6 21.2 %multiply_convert_fusion.2 = bf16[4,6,256,1024]{3,2,1,0:T(8,128)(2,1)} fusion(f32[4,6,256,1024]{3,2,1,0:T(8,128)} %get-tuple-element.431, f32[4,6,256,1024]{3,2,1,0:T(8,128)} %fusion.160, f32[4,6,256]{2,1,0:T(8,128)S(1)} %get-tuple-element.432), kind=kLoop, calls=%fused_computation.15.clone.1 | loop fusion | flops 18874368 | bytes 62939136 | tf_op jit(solution)/shard_map/while/body/eval_jaxpr/convert_element_type | solution.py:106
  726.1 20.0 %multiply_reduce_fusion.7 = (f32[4,6,256]{2,1,0:T(8,128)S(1)}, f32[4,6,256,1024]{3,2,1,0:T(8,128)}) fusion(f32[4,6,256,1024]{3,2,1,0:T(8,128)} %fusion.160, f32[4,6,256]{2,1,0:T(8,128)S(1)} %get-tuple-element.429, f32[4,6,256]{2,1,0:T(8,128)S(1)} %get-tuple-element.430, bf16[4,256,6,64]{1,3,2,0:T(8,128)(2,1)S(1)} %bitcast.187, ...), kind=kOutput, calls=%fused_computation.16.clone.1 | convolution fusion | flops 843048960 | bytes 55386112 | tf_op jit(solution)/shard_map/while/body/eval_jaxpr/gqhd,gkhd->ghqk/dot_general | solution.py:68
  746.2 21.2 %multiply_convert_fusion.2 = bf16[4,6,256,1024]{3,2,1,0:T(8,128)(2,1)} fusion(f32[4,6,256,1024]{3,2,1,0:T(8,128)} %get-tuple-element.431, f32[4,6,256,1024]{3,2,1,0:T(8,128)} %fusion.160, f32[4,6,256]{2,1,0:T(8,128)S(1)} %get-tuple-element.432), kind=kLoop, calls=%fused_computation.15.clone.1 | loop fusion | flops 18874368 | bytes 62939136 | tf_op jit(solution)/shard_map/while/body/eval_jaxpr/convert_element_type | solution.py:106
  833.5 53.9 %reduce-scatter.20.cloned.1.call-done = bf16[8,256,384]{2,1,0:T(8,128)(2,1)} async-done(((bf16[8,1024,384]{2,1,0:T(8,128)(2,1)}), bf16[8,256,384]{2,1,0:T(8,128)(2,1)}) %reduce-scatter.20.cloned.1.call-update) | async-done | bytes 1572880 | tf_op jit(solution)/shard_map/reduce_scatter | solution.py:330
  897.3 63.5 %reduce-scatter.22.cloned.1.call-done = bf16[8,256,384]{2,1,0:T(8,128)(2,1)} async-done(((bf16[8,1024,384]{2,1,0:T(8,128)(2,1)}), bf16[8,256,384]{2,1,0:T(8,128)(2,1)}) %reduce-scatter.22.cloned.1.call-update) | async-done | bytes 1572880 | tf_op jit(solution)/shard_map/reduce_scatter | solution.py:333
  1022.0 75.8 %all-reduce.22 = (f32[768]{0:T(1024)S(1)}, f32[3072]{0:T(1024)S(1)}, f32[768]{0:T(1024)S(1)}, f32[768]{0:T(1024)S(1)}, f32[768]{0:T(1024)S(1)}, /*index=5*/f32[768]{0:T(1024)S(1)}, f32[768]{0:T(1024)S(1)}) all-reduce(f32[768]{0:T(1024)S(1)} %fusion.62, ...), channel_id=15, replica_groups=mesh['shard'=4,'ctx'=4,'tp'=2] {'shard','ctx'}, use_global_device_ids=true, to_apply=%region_30.31.clone | all-reduce | flops 7680 | bytes 61440
  1107.6 140.2 %reduce-scatter.32.cloned.1.call-done = f32[1536,48]{0,1:T(8,128)} async-done(((f32[1536,768]{0,1:T(8,128)}), f32[1536,48]{0,1:T(8,128)}) %reduce-scatter.32.cloned.1.call-update) | async-done | bytes 294928 | tf_op jit(solution)/shard_map/reduce_scatter | solution.py:412
  1247.8 141.4 %reduce-scatter.30.cloned.1.call-done = f32[48,1536]{1,0:T(8,128)} async-done(((f32[768,1536]{1,0:T(8,128)}), f32[48,1536]{1,0:T(8,128)}) %reduce-scatter.30.cloned.1.call-update) | async-done | bytes 294928 | tf_op jit(solution)/shard_map/reduce_scatter | solution.py:411
  1389.1 128.9 %reduce-scatter.28.cloned.1.call-done = f32[384,48]{0,1:T(8,128)} async-done(((f32[384,768]{0,1:T(8,128)}), f32[384,48]{0,1:T(8,128)}) %reduce-scatter.28.cloned.1.call-update) | async-done | bytes 73744 | tf_op jit(solution)/shard_map/reduce_scatter | solution.py:410
  1518.0 138.8 %reduce-scatter.26.cloned.1.call-done = f32[48,3,384]{2,0,1:T(8,128)} async-done(((f32[768,3,384]{2,0,1:T(8,128)}), f32[48,3,384]{2,0,1:T(8,128)}) %reduce-scatter.26.cloned.1.call-update) | async-done | bytes 221200 | tf_op jit(solution)/shard_map/reduce_scatter | solution.py:409
  (364 shorter events, 452.6 us)
Async XLA Ops:
  7.2 65.2 %all-gather.13.cloned.1.call-start = ((), (), s32[]{:S(2)}) async-start(), calls=%async_computation.12 | async-start | bytes 1880064 | tf_op jit(solution)/shard_map/all_gather | solution.py:200
  7.9 76.9 %all-gather.11.cloned.1.call-start = ((), (), s32[]{:S(2)}) async-start(), calls=%async_computation.11 | async-start | bytes 4718592 | tf_op jit(solution)/shard_map/all_gather | solution.py:233
  8.7 173.3 %all-gather.15.cloned.1.call-start = ((), (), s32[]{:S(2)}) async-start(), calls=%async_computation.13 | async-start | bytes 7864320 | tf_op jit(solution)/shard_map/all_gather | solution.py:246
  96.0 155.0 %all-gather.17.cloned.1.call-start = ((), (), s32[]{:S(2)}) async-start(), calls=%async_computation.14 | async-start | bytes 7864320 | tf_op jit(solution)/shard_map/all_gather | solution.py:245
  125.8 305.2 %reduce-scatter.14.cloned.1.call-start = ((), (), s32[]{:S(2)}) async-start(), calls=%async_computation.15 | async-start | bytes 4718592 | tf_op jit(solution)/shard_map/reduce_scatter | solution.py:261
  350.2 86.8 %all-gather.21.cloned.1.call-start = ((), (), s32[]{:S(2)}) async-start(), calls=%async_computation.17 | async-start | bytes 2506752 | tf_op jit(solution)/shard_map/all_gather | solution.py:202
  350.8 93.5 %all-gather.19.cloned.1.call-start = ((), (), s32[]{:S(2)}) async-start(), calls=%async_computation.16 | async-start | bytes 4718592 | tf_op jit(solution)/shard_map/all_gather | solution.py:269
  431.0 160.1 %copy-start.37 = (f32[768]{0:T(1024)}, f32[768]{0:T(1024)S(1)}, u32[]{:S(2)}) copy-start(f32[768]{0:T(1024)S(1)} %convert_element_type.190) | copy-start | bytes 9220
  431.0 160.1 %copy-start.41 = (f32[768]{0:T(1024)}, f32[768]{0:T(1024)S(1)}, u32[]{:S(2)}) copy-start(f32[768]{0:T(1024)S(1)} %convert_element_type.191) | copy-start | bytes 9220
  433.2 157.9 %copy-start.39 = (f32[8,128]{1,0:T(8,128)}, f32[8,128]{1,0:T(8,128)S(1)}, u32[]{:S(2)}) copy-start(f32[8,128]{1,0:T(8,128)S(1)} %broadcast_multiply_fusion.6) | copy-start | bytes 12292
  434.0 157.1 %copy-start.43 = (f32[8,128]{1,0:T(8,128)}, f32[8,128]{1,0:T(8,128)S(1)}, u32[]{:S(2)}) copy-start(f32[8,128]{1,0:T(8,128)S(1)} %add_rsqrt_fusion.1) | copy-start | bytes 12292
  436.1 74.8 %all-gather.23.cloned.1.call-start = ((), (), s32[]{:S(2)}) async-start(), calls=%async_computation.18 | async-start | bytes 2506752 | tf_op jit(solution)/shard_map/all_gather | solution.py:203
  436.9 93.0 %reduce-scatter.16.cloned.1.call-start = ((), (), s32[]{:S(2)}) async-start(), calls=%async_computation.19 | async-start | bytes 4718592 | tf_op jit(solution)/shard_map/reduce_scatter | solution.py:278
  520.0 33.3 %all-gather.25.cloned.1.call-start = ((), (), s32[]{:S(2)}) async-start(), calls=%async_computation.20 | async-start | bytes 4718592 | tf_op jit(solution)/shard_map/all_gather | solution.py:290
  539.8 44.5 %reduce-scatter.18.cloned.1.call-start = ((), (), s32[]{:S(2)}) async-start(), calls=%async_computation.21 | async-start | bytes 4718592 | tf_op jit(solution)/shard_map/reduce_scatter | solution.py:296
  572.1 35.3 %all-gather.27.cloned.1.call-start = ((), (), s32[]{:S(2)}) async-start(), calls=%async_computation.22 | async-start | bytes 4718592 | tf_op jit(solution)/shard_map/all_gather | solution.py:304
  594.0 293.4 %reduce-scatter.20.cloned.1.call-start = ((), (), s32[]{:S(2)}) async-start(), calls=%async_computation.23 | async-start | bytes 7864320 | tf_op jit(solution)/shard_map/reduce_scatter | solution.py:330
  815.9 144.9 %reduce-scatter.22.cloned.1.call-start = ((), (), s32[]{:S(2)}) async-start(), calls=%async_computation.24 | async-start | bytes 7864320 | tf_op jit(solution)/shard_map/reduce_scatter | solution.py:333
  824.6 277.3 %reduce-scatter.34.cloned.1.call-start = ((), (), s32[]{:S(2)}) async-start(), calls=%async_computation.30 | async-start | bytes 417792
  968.9 134.4 %reduce-scatter.24.cloned.1.call-start = ((), (), s32[]{:S(2)}) async-start(), calls=%async_computation.25 | async-start | bytes 4718592 | tf_op jit(solution)/shard_map/reduce_scatter | solution.py:355
  976.8 271.0 %reduce-scatter.32.cloned.1.call-start = ((), (), s32[]{:S(2)}) async-start(), calls=%async_computation.29 | async-start | bytes 5013504 | tf_op jit(solution)/shard_map/reduce_scatter | solution.py:412
  987.0 402.1 %reduce-scatter.30.cloned.1.call-start = ((), (), s32[]{:S(2)}) async-start(), calls=%async_computation.28 | async-start | bytes 5013504 | tf_op jit(solution)/shard_map/reduce_scatter | solution.py:411
  996.9 521.1 %reduce-scatter.28.cloned.1.call-start = ((), (), s32[]{:S(2)}) async-start(), calls=%async_computation.27 | async-start | bytes 1253376 | tf_op jit(solution)/shard_map/reduce_scatter | solution.py:410
  1002.3 654.5 %reduce-scatter.26.cloned.1.call-start = ((), (), s32[]{:S(2)}) async-start(), calls=%async_computation.26 | async-start | bytes 3760128 | tf_op jit(solution)/shard_map/reduce_scatter | solution.py:409
  (71 other events, 1586.6 us)
Sparse Core Ops, SparseCore 0:
  10.7 61.6 all-gather.12
  73.9 10.8 all-gather.10
  96.2 82.8 all-gather.14
  180.8 70.1 all-gather.16
  350.3 10.8 reduce-scatter.13
  364.3 63.8 all-gather.20
  436.2 7.9 all-gather.18
  447.4 63.4 all-gather.22
  520.1 9.7 reduce-scatter.15
  540.0 13.2 all-gather.24
  572.2 12.0 reduce-scatter.17
  594.1 13.2 all-gather.26
  816.0 71.3 reduce-scatter.19
  890.6 70.1 reduce-scatter.21
  969.0 121.6 reduce-scatter.33
  1092.8 9.9 reduce-scatter.23
  1109.2 138.5 reduce-scatter.31
  1253.4 135.7 reduce-scatter.29
  1395.2 122.8 reduce-scatter.27
  1524.4 132.4 reduce-scatter.25
where the time goes:
time: 1670 us; the launch traced here: 1660 us
  waiting for transfers between devices  848 us (51%)
  matrix products  282 us (17%)
  blocking collectives  247 us (15%)
  local copies, waits for them, and re-layouts  143 us (9%)
  other arithmetic  123 us (7%)
  between operations  18.3 us (1%)
    unnamed x3, blocking collectives  156 us
    reduce_scatter x1, waiting for transfers between devices, local(): lax.psum_scatter(up_weight_grad, ('shard', 'ctx'), scatter_dimension=0, t...  141 us
    reduce_scatter x1, waiting for transfers between devices, local(): lax.psum_scatter(down_weight_grad, ('shard', 'ctx'), scatter_dimension=1,...  140 us
    reduce_scatter x1, waiting for transfers between devices, local(): lax.psum_scatter(project_weight_grad, ('shard', 'ctx'), scatter_dimension...  139 us
    reduce_scatter x1, waiting for transfers between devices, local(): lax.psum_scatter(attend_weight_grad, ('shard', 'ctx'), scatter_dimension=...  129 us
    reduce_scatter x1, waiting for transfers between devices, local(): lax.psum_scatter(ungroup(value_part).astype(jnp.bfloat16), 'ctx', scatter...  63.5 us
    dot_general x4, matrix products, head_scores(): jnp.einsum('gqhd,gkhd->ghqk', split_heads(queries, heads), split_heads(ke...  61.4 us
    all_gather x1, waiting for transfers between devices, local(): lax.all_gather(key_rot, 'ctx', axis=1, tiled=True)  60.3 us
  transfers between devices with their start and end apart: 20, of which 15 were waited for; matrix products, arithmetic and copies ran while one was open for 10% of the time, Pallas kernels for 0%

commit v1 on v0

v1 whole, which is shorter than its diff:
```python
import math

import jax
import jax.numpy as jnp
from jax import lax
from jax.experimental import pallas as pl
from jax.experimental.pallas import tpu as pltpu
from jax.sharding import PartitionSpec as P

D = 768
HEADS = 12
HEAD_DIM = 64
FF = 3072
S = 1024
LANES = 128
PAIRS = HEADS // 2
Q_ROWS = 128
K_ROWS = 256

norm_eps = 1e-12
mask_fill = -1000000000.0

NT = (((1,), (1,)), ((), ()))
TN = (((0,), (0,)), ((), ()))
NN = (((1,), (0,)), ((), ()))


def dot(left, right, dims):
    return lax.dot_general(left, right, dims, preferred_element_type=jnp.float32)


def swap_pairs(values):
    lane = lax.broadcasted_iota(jnp.int32, values.shape, 1)
    width = values.shape[1]
    return jnp.where(
        lane % 2 == 0, -pltpu.roll(values, width - 1, 1), pltpu.roll(values, 1, 1)
    )


def stack_heads(rows):
    lane = lax.broadcasted_iota(jnp.int32, rows.shape, 1)
    zero = jnp.zeros_like(rows)
    return jnp.concatenate(
        [jnp.where(lane < HEAD_DIM, rows, zero), jnp.where(lane < HEAD_DIM, zero, rows)], axis=0
    )


def pick_heads(both):
    return jnp.concatenate([both[:HEAD_DIM, :Q_ROWS], both[HEAD_DIM:, Q_ROWS:]], axis=0)


def spread_heads(row):
    return jnp.concatenate(
        [
            jnp.broadcast_to(row[:, :Q_ROWS], (HEAD_DIM, Q_ROWS)),
            jnp.broadcast_to(row[:, Q_ROWS:], (HEAD_DIM, Q_ROWS)),
        ],
        axis=0,
    )


def mask_bias(key_code, query_low, query_high):
    keys = jnp.broadcast_to(key_code, (K_ROWS, Q_ROWS))
    allowed = (keys >= query_low) & (keys <= query_high)
    bias = jnp.where(allowed, 0.0, mask_fill)
    return jnp.concatenate([bias, bias], axis=1)


def attend_kernel(
    first_ref, count_ref, x_ref, w_ref, b_ref, cos_ref, sin_ref, code_ref, low_ref, high_ref,
    q_ref, k_ref, v_ref, o_ref, lse_ref, top, total, acc, stacked,
):
    own = pl.program_id(0)
    row_tile = 256

    @pl.loop(0, S // row_tile)
    def _(tile):
        rows = pl.ds(pl.multiple_of(tile * row_tile, row_tile), row_tile)
        x = x_ref[rows, :]
        cosine = cos_ref[rows, :]
        sine = sin_ref[rows, :]
        for part, out in enumerate((q_ref, k_ref, v_ref)):
            joint = dot(x, w_ref[part], NN) + b_ref[pl.ds(part, 1), :]
            for pair in range(PAIRS):
                lanes = slice(pair * LANES, (pair + 1) * LANES)
                piece = joint[:, lanes]
                if part < 2:
                    piece = piece * cosine + swap_pairs(piece) * sine
                if part == 0:
                    piece = piece.astype(jnp.bfloat16) * jnp.asarray(HEAD_DIM**-0.5, jnp.bfloat16)
                out[rows, lanes] = piece.astype(jnp.bfloat16)

    @pl.loop(0, S // Q_ROWS)
    def _(block):
        start = pl.multiple_of(block * Q_ROWS, Q_ROWS)
        rows = pl.ds(start, Q_ROWS)
        for pair in range(PAIRS):
            stacked[pair] = stack_heads(q_ref[rows, pair * LANES : (pair + 1) * LANES])
        top[...] = jnp.full_like(top, 2.0 * mask_fill)
        total[...] = jnp.zeros_like(total)
        acc[...] = jnp.zeros_like(acc)
        low = low_ref[:, rows]
        high = high_ref[:, rows]

        @pl.loop(0, count_ref[own, block])
        def _(step):
            window = pl.ds(pl.multiple_of(first_ref[own, block] + step * K_ROWS, 16), K_ROWS)
            bias = mask_bias(code_ref[window, :], low, high)
            for pair in range(PAIRS):
                lanes = slice(pair * LANES, (pair + 1) * LANES)
                scores = dot(k_ref[window, lanes], stacked[pair], NT) + bias
                old = top[pair]
                new = jnp.maximum(old, jnp.max(scores, axis=0, keepdims=True))
                expo = jnp.exp(scores - new)
                fade = jnp.exp(old - new)
                top[pair] = new
                total[pair] = total[pair] * fade + jnp.sum(expo, axis=0, keepdims=True)
                mixed = dot(v_ref[window, lanes], expo.astype(jnp.bfloat16), TN)
                acc[pair] = acc[pair] * spread_heads(fade) + pick_heads(mixed)

        for pair in range(PAIRS):
            lanes = slice(pair * LANES, (pair + 1) * LANES)
            summed = total[pair]
            out = acc[pair] / spread_heads(summed)
            o_ref[rows, lanes] = jnp.transpose(out).astype(jnp.bfloat16)
            lse = top[pair] + jnp.log(summed)
            lse_ref[pl.ds(2 * pair, 1), rows] = lse[:, :Q_ROWS]
            lse_ref[pl.ds(2 * pair + 1, 1), rows] = lse[:, Q_ROWS:]


def attend_back_kernel(
    first_ref, count_ref, q_ref, k_ref, v_ref, o_ref, g_ref, lse_ref, cos_ref, sin_ref, code_ref,
    low_ref, high_ref, joint_ref, acc, keys, values, stacked, grads, delta, level,
):
    own = pl.program_id(0)
    keys[...] = jnp.zeros_like(keys)
    values[...] = jnp.zeros_like(values)

    @pl.loop(0, S // Q_ROWS)
    def _(block):
        start = pl.multiple_of(block * Q_ROWS, Q_ROWS)
        rows = pl.ds(start, Q_ROWS)
        for pair in range(PAIRS):
            lanes = slice(pair * LANES, (pair + 1) * LANES)
            stacked[pair] = stack_heads(q_ref[rows, lanes])
            grad = g_ref[rows, lanes]
            grads[pair] = stack_heads(grad)
            both = jnp.transpose(grad.astype(jnp.float32) * o_ref[rows, lanes].astype(jnp.float32))
            delta[pair] = jnp.concatenate(
                [
                    jnp.sum(both[:HEAD_DIM], axis=0, keepdims=True),
                    jnp.sum(both[HEAD_DIM:], axis=0, keepdims=True),
                ],
                axis=1,
            )
            level[pair] = jnp.concatenate(
                [lse_ref[pl.ds(2 * pair, 1), rows], lse_ref[pl.ds(2 * pair + 1, 1), rows]], axis=1
            )
        acc[...] = jnp.zeros_like(acc)
        low = low_ref[:, rows]
        high = high_ref[:, rows]

        @pl.loop(0, count_ref[own, block])
        def _(step):
            window = pl.ds(pl.multiple_of(first_ref[own, block] + step * K_ROWS, 16), K_ROWS)
            bias = mask_bias(code_ref[window, :], low, high)
            for pair in range(PAIRS):
                lanes = slice(pair * LANES, (pair + 1) * LANES)
                query = stacked[pair]
                grad = grads[pair]
                key = k_ref[window, lanes]
                scores = dot(key, query, NT) + bias
                probs = jnp.exp(scores - level[pair])
                prob_grad = dot(v_ref[window, lanes], grad, NT)
                score_grad = (probs * (prob_grad - delta[pair])).astype(jnp.bfloat16)
                values[window, lanes] += dot(probs.astype(jnp.bfloat16), grad, NN)
                keys[window, lanes] += dot(score_grad, query, NN)
                acc[pair] += pick_heads(dot(key, score_grad, TN))

        cosine = cos_ref[rows, :]
        sine = sin_ref[rows, :]
        for pair in range(PAIRS):
            lanes = slice(pair * LANES, (pair + 1) * LANES)
            query = jnp.transpose(acc[pair]) * (HEAD_DIM**-0.5)
            joint_ref[rows, lanes] = (query * cosine - swap_pairs(query) * sine).astype(jnp.bfloat16)

    @pl.loop(0, S // Q_ROWS)
    def _(block):
        rows = pl.ds(pl.multiple_of(block * Q_ROWS, Q_ROWS), Q_ROWS)
        cosine = cos_ref[rows, :]
        sine = sin_ref[rows, :]
        for pair in range(PAIRS):
            lanes = slice(pair * LANES, (pair + 1) * LANES)
            key = keys[rows, lanes]
            joint_ref[rows, D + pair * LANES : D + (pair + 1) * LANES] = (
                key * cosine - swap_pairs(key) * sine
            ).astype(jnp.bfloat16)
            joint_ref[rows, 2 * D + pair * LANES : 2 * D + (pair + 1) * LANES] = values[
                rows, lanes
            ].astype(jnp.bfloat16)


def whole(*shape):
    return pl.BlockSpec(shape, lambda i, *_: (0,) * len(shape))


def per(*shape):
    return pl.BlockSpec((None,) + shape, lambda i, *_: (i,) + (0,) * len(shape))


def attend(first, count, x, weight, bias, cosine, sine, code, low, high):
    own = x.shape[0]
    act = jax.ShapeDtypeStruct((own, S, D), jnp.bfloat16)
    return pl.pallas_call(
        attend_kernel,
        grid_spec=pltpu.PrefetchScalarGridSpec(
            num_scalar_prefetch=2,
            grid=(own,),
            in_specs=[
                per(S, D), whole(3, D, D), whole(3, D), whole(S, LANES), whole(S, LANES),
                per(S, 1), per(1, S), per(1, S),
            ],
            out_specs=[per(S, D), per(S, D), per(S, D), per(S, D), per(HEADS, S)],
            scratch_shapes=[
                pltpu.VMEM((PAIRS, 1, 2 * Q_ROWS), jnp.float32),
                pltpu.VMEM((PAIRS, 1, 2 * Q_ROWS), jnp.float32),
                pltpu.VMEM((PAIRS, LANES, Q_ROWS), jnp.float32),
                pltpu.VMEM((PAIRS, 2 * Q_ROWS, LANES), jnp.bfloat16),
            ],
        ),
        out_shape=[act, act, act, act, jax.ShapeDtypeStruct((own, HEADS, S), jnp.float32)],
        compiler_params=pltpu.CompilerParams(vmem_limit_bytes=60 << 20),
        name="attend",
        cost_estimate=pl.CostEstimate(flops=6 * 10**9, bytes_accessed=12 << 20, transcendentals=6 << 20),
    )(first, count, x, weight, bias, cosine, sine, code, low, high)


def attend_back(first, count, q, k, v, o, g, lse, cosine, sine, code, low, high):
    own = q.shape[0]
    return pl.pallas_call(
        attend_back_kernel,
        grid_spec=pltpu.PrefetchScalarGridSpec(
            num_scalar_prefetch=2,
            grid=(own,),
            in_specs=[
                per(S, D), per(S, D), per(S, D), per(S, D), per(S, D), per(HEADS, S),
                whole(S, LANES), whole(S, LANES), per(S, 1), per(1, S), per(1, S),
            ],
            out_specs=per(S, 3 * D),
            scratch_shapes=[
                pltpu.VMEM((PAIRS, LANES, Q_ROWS), jnp.float32),
                pltpu.VMEM((S, D), jnp.float32),
                pltpu.VMEM((S, D), jnp.float32),
                pltpu.VMEM((PAIRS, 2 * Q_ROWS, LANES), jnp.bfloat16),
                pltpu.VMEM((PAIRS, 2 * Q_ROWS, LANES), jnp.bfloat16),
                pltpu.VMEM((PAIRS, 1, 2 * Q_ROWS), jnp.float32),
                pltpu.VMEM((PAIRS, 1, 2 * Q_ROWS), jnp.float32),
            ],
        ),
        out_shape=jax.ShapeDtypeStruct((own, S, 3 * D), jnp.bfloat16),
        compiler_params=pltpu.CompilerParams(vmem_limit_bytes=60 << 20),
        name="attend_back",
        cost_estimate=pl.CostEstimate(flops=12 * 10**9, bytes_accessed=14 << 20, transcendentals=6 << 20),
    )(first, count, q, k, v, o, g, lse, cosine, sine, code, low, high)


def mask_tables(segments, padding):
    code = 2 * segments + padding
    low = code
    high = 2 * segments + 1
    blocks = segments.reshape(segments.shape[0], S // Q_ROWS, Q_ROWS)
    begin = jnp.sum(segments[:, None, :] < blocks[:, :, :1], axis=-1, dtype=jnp.int32)
    end = jnp.sum(segments[:, None, :] <= blocks[:, :, -1:], axis=-1, dtype=jnp.int32)
    begin = begin // 16 * 16
    count = (end - begin + K_ROWS - 1) // K_ROWS
    first = jnp.minimum(begin, S - count * K_ROWS)
    return first, count, code[:, :, None], low[:, None, :], high[:, None, :]


def angles():
    position = jnp.arange(S, dtype=jnp.int32).astype(jnp.float32)
    column = jnp.arange(LANES, dtype=jnp.int32) % HEAD_DIM // 2
    rate = jnp.exp(column.astype(jnp.float32) * (-2.0 * math.log(10000.0) / HEAD_DIM))
    phase = position[:, None] * rate[None, :]
    return jnp.cos(phase), jnp.sin(phase)


def normalize(rows, gain, shift):
    mean = jnp.mean(rows, axis=-1, keepdims=True)
    centred = rows - mean
    factor = lax.rsqrt(jnp.mean(centred * centred, axis=-1, keepdims=True) + norm_eps)
    unit = centred * factor
    return (unit * gain + shift, unit, factor)


def normalize_back(incoming, unit, factor, gain):
    gain_grad = jnp.sum(incoming * unit, axis=0)
    shift_grad = jnp.sum(incoming, axis=0)
    inner = incoming * gain
    rows_grad = factor * (
        inner
        - jnp.mean(inner, axis=-1, keepdims=True)
        - unit * jnp.mean(inner * unit, axis=-1, keepdims=True)
    )
    return (rows_grad, gain_grad, shift_grad)


def gelu_slope(values):
    cumulative = 0.5 * (1.0 + lax.erf(values * (1.0 / math.sqrt(2.0))))
    density = jnp.exp(-0.5 * values * values) * (1.0 / math.sqrt(2.0 * math.pi))
    return cumulative + values * density


ROWS = ("shard", "ctx")
EVERY = ("shard", "ctx", "tp")
SEQ = ("ctx", "tp")


def local(
    tokens, project_weight, attend_weight, up_weight, down_weight, project_bias, attend_bias,
    up_bias, down_bias, first_gain, first_shift, second_gain, second_shift, segment_ids, padding,
    cotangent,
):
    seq_count = tokens.shape[0]
    members = lax.axis_size("ctx") * lax.axis_size("tp")
    own = seq_count // members
    rank = lax.axis_index("ctx") * lax.axis_size("tp") + lax.axis_index("tp")
    rows = own * S
    pieces = lax.axis_size("shard") * lax.axis_size("ctx")
    depth = D // pieces

    def to_sequences(array):
        return lax.all_to_all(array, SEQ, 0, 1, tiled=True)

    def to_blocks(array):
        return lax.all_to_all(array, SEQ, 1, 0, tiled=True)

    x = to_sequences(tokens)
    segments = lax.dynamic_slice_in_dim(segment_ids, rank * own, own, 0)
    pads = lax.dynamic_slice_in_dim(padding, rank * own, own, 0)

    def gather(shard, axis):
        part = lax.all_gather(shard, ROWS, axis=axis, tiled=True)
        return lax.all_gather(part, "tp", axis=axis + 1, tiled=True)

    project = gather(jnp.transpose(project_weight, (1, 0, 2)), 1)
    attend_t = gather(jnp.transpose(attend_weight), 0)
    up = gather(up_weight, 0)
    down_t = gather(jnp.transpose(down_weight), 0)

    vectors = jnp.concatenate(
        [
            project_bias,
            attend_bias[None],
            down_bias[None],
            first_gain[None],
            first_shift[None],
            second_gain[None],
            second_shift[None],
            up_bias.reshape(FF // D, depth),
        ],
        axis=0,
    )
    vectors = lax.all_gather(vectors, ROWS, axis=0).astype(jnp.float32)
    wide = jnp.transpose(vectors[:, :9], (1, 0, 2)).reshape(9, D)
    up_shift = vectors[:, 9:].reshape(FF)

    tables = mask_tables(segments, pads)
    cosine, sine = angles()
    query, key, value, attended, level = attend(
        tables[0], tables[1], x, project, wide[:3], cosine, sine, *tables[2:]
    )
    flat = x.reshape(rows, D)
    attended_flat = attended.reshape(rows, D)
    branch = dot(attended_flat, attend_t, NT) + wide[3]
    first, first_unit, first_factor = normalize(flat.astype(jnp.float32) + branch, wide[5], wide[6])
    first_low = first.astype(jnp.bfloat16)
    pre = dot(first_low, up, NN) + up_shift
    hidden = jax.nn.gelu(pre, approximate=False).astype(jnp.bfloat16)
    ffn = dot(hidden, down_t, NT) + wide[4]
    second, second_unit, second_factor = normalize(first + ffn, wide[7], wide[8])
    output = to_blocks(second.astype(jnp.bfloat16).reshape(own, S, D))

    incoming = to_sequences(cotangent).reshape(rows, D).astype(jnp.float32)
    second_grad, second_gain_grad, second_shift_grad = normalize_back(
        incoming, second_unit, second_factor, wide[7]
    )
    ffn_grad = second_grad.astype(jnp.bfloat16)
    down_bias_grad = jnp.sum(ffn_grad.astype(jnp.float32), axis=0)
    down_t_grad = dot(ffn_grad, hidden, TN)
    pre_grad = (dot(ffn_grad, down_t, NN) * gelu_slope(pre)).astype(jnp.bfloat16)
    up_bias_grad = jnp.sum(pre_grad.astype(jnp.float32), axis=0)
    up_grad = dot(first_low, pre_grad, TN)
    first_total = second_grad + dot(pre_grad, up, NT)
    first_grad, first_gain_grad, first_shift_grad = normalize_back(
        first_total, first_unit, first_factor, wide[5]
    )
    branch_grad = first_grad.astype(jnp.bfloat16)
    attend_bias_grad = jnp.sum(branch_grad.astype(jnp.float32), axis=0)
    attend_t_grad = dot(branch_grad, attended_flat, TN)
    attended_grad = dot(branch_grad, attend_t, NN).astype(jnp.bfloat16)

    joint_grad = attend_back(
        tables[0], tables[1], query, key, value, attended, attended_grad.reshape(own, S, D), level,
        cosine, sine, *tables[2:],
    ).reshape(rows, 3 * D)
    project_bias_grad = jnp.sum(joint_grad.astype(jnp.float32), axis=0).reshape(3, D)
    project_grad = jnp.stack(
        [dot(flat, joint_grad[:, i * D : (i + 1) * D], TN) for i in range(3)]
    )
    token_part = sum(
        dot(joint_grad[:, i * D : (i + 1) * D], project[i], NT) for i in range(3)
    )
    tokens_grad = to_blocks((first_grad + token_part).astype(jnp.bfloat16).reshape(own, S, D))

    def scatter(grad, axis):
        part = lax.psum_scatter(
            grad.astype(jnp.bfloat16), "tp", scatter_dimension=axis + 1, tiled=True
        )
        return lax.psum_scatter(part, ROWS, scatter_dimension=axis, tiled=True).astype(jnp.float32)

    sums = jnp.concatenate(
        [
            project_bias_grad,
            attend_bias_grad[None],
            down_bias_grad[None],
            first_gain_grad[None],
            first_shift_grad[None],
            second_gain_grad[None],
            second_shift_grad[None],
        ],
        axis=0,
    )
    sums = jnp.concatenate(
        [
            jnp.transpose(sums.reshape(9, pieces, depth), (1, 0, 2)),
            up_bias_grad.reshape(pieces, FF // D, depth),
        ],
        axis=1,
    )
    sums = lax.psum(sums, EVERY)
    mine = lax.axis_index("shard") * lax.axis_size("ctx") + lax.axis_index("ctx")
    sums = lax.dynamic_index_in_dim(sums, mine, 0, keepdims=False)
    return (
        output,
        tokens_grad,
        jnp.transpose(scatter(project_grad, 1), (1, 0, 2)),
        jnp.transpose(scatter(attend_t_grad, 0)),
        scatter(up_grad, 0),
        jnp.transpose(scatter(down_t_grad, 0)),
        sums[:3],
        sums[3],
        sums[9:].reshape(-1),
        sums[4],
        sums[5],
        sums[6],
        sums[7],
        sums[8],
    )


def solution(mesh):
    in_specs = (
        P("shard", ("ctx", "tp"), None),
        P(("shard", "ctx"), None, "tp"),
        P("tp", ("shard", "ctx")),
        P(("shard", "ctx"), "tp"),
        P("tp", ("shard", "ctx")),
        P(None, ("shard", "ctx")),
        P(("shard", "ctx")),
        P(("shard", "ctx")),
        P(("shard", "ctx")),
        P(("shard", "ctx")),
        P(("shard", "ctx")),
        P(("shard", "ctx")),
        P(("shard", "ctx")),
        P("shard", None),
        P("shard", None),
        P("shard", ("ctx", "tp"), None),
    )
    out_specs = (
        P("shard", ("ctx", "tp"), None),
        P("shard", ("ctx", "tp"), None),
        P(("shard", "ctx"), None, "tp"),
        P("tp", ("shard", "ctx")),
        P(("shard", "ctx"), "tp"),
        P("tp", ("shard", "ctx")),
        P(None, ("shard", "ctx")),
        P(("shard", "ctx")),
        P(("shard", "ctx")),
        P(("shard", "ctx")),
        P(("shard", "ctx")),
        P(("shard", "ctx")),
        P(("shard", "ctx")),
        P(("shard", "ctx")),
    )
    return jax.shard_map(local, mesh=mesh, in_specs=in_specs, out_specs=out_specs, check_vma=False)
```

time: 1670 us -> 1020 us (0.61)
  waiting for transfers between devices: 848 us -> 509 us
  matrix products: 282 us -> 123 us
  blocking collectives: 247 us -> 150 us
  Pallas kernels: 0 us -> 89.5 us
  local copies, waits for them, and re-layouts: 143 us -> 62.6 us
  other arithmetic: 123 us -> 48.9 us
    reduce_scatter x10 -> x6, waiting for transfers between devices: 688 us -> 279 us  [the longest x3 266 us: scatter(): lax.psum_scatter(part, ROWS, scatter_dimension=axis, tiled=True)]
    dot_general x26 -> x15, matrix products: 282 us -> 123 us  [dot(): lax.dot_general(left, right, dims, preferred_element_type=jnp.float32)]
    unnamed x3 -> x0, blocking collectives: 156 us -> none
    unnamed x21 -> x17, waiting for transfers between devices: 2.86 us -> 138 us
    pallas_call x0 -> x2, Pallas kernels: none -> 89.5 us  [the longest x1 45.8 us: attend(): pl.pallas_call(attend_kernel, grid_spec=pltpu.PrefetchScalarGridSpec(num_...]
    all_gather x9 -> x7, waiting for transfers between devices: 157 us -> 82.1 us  [the longest x3 82.1 us: gather(): part = lax.all_gather(shard, ROWS, axis=axis, tiled=True)]
    convert_element_type x13 -> x3, other arithmetic: 58.9 us -> 1.66 us  [the longest x1 1.64 us: scatter(): lax.psum_scatter(part, ROWS, scatter_dimension=axis, tiled=True)]
    psum x0 -> x1, blocking collectives: none -> 51.7 us  [local(): sums = lax.psum(sums, EVERY)]
  transfers between devices with their start and end apart: 20 -> 19, of which waited for: 15 -> 8; matrix products, arithmetic and copies ran while one was open for 10% -> 18% of each run, Pallas kernels for 0% -> 9%
where the time goes in v1:
time: 1020 us
  waiting for transfers between devices  509 us (50%)
  blocking collectives  150 us (15%)
  matrix products  123 us (12%)
  Pallas kernels  89.5 us (9%)
  local copies, waits for them, and re-layouts  62.6 us (6%)
  other arithmetic  48.9 us (5%)
  starting transfers between devices  16.9 us (2%)
  between operations  15.4 us (2%)
    reduce_scatter x3, waiting for transfers between devices, scatter(): lax.psum_scatter(part, ROWS, scatter_dimension=axis, tiled=True)  266 us
    unnamed x17, waiting for transfers between devices  138 us
    dot_general x15, matrix products, dot(): lax.dot_general(left, right, dims, preferred_element_type=jnp.float32)  123 us
    all_gather x3, waiting for transfers between devices, gather(): part = lax.all_gather(shard, ROWS, axis=axis, tiled=True)  82.1 us
    all_gather x1, blocking collectives, local(): vectors = lax.all_gather(vectors, ROWS, axis=0).astype(jnp.float32)  52.2 us
    psum x1, blocking collectives, local(): sums = lax.psum(sums, EVERY)  51.7 us
    all_gather x1, blocking collectives, gather(): part = lax.all_gather(shard, ROWS, axis=axis, tiled=True)  46.2 us
    pallas_call x1, Pallas kernels, attend(): pl.pallas_call(attend_kernel, grid_spec=pltpu.PrefetchScalarGridSpec(num_...  45.8 us
  transfers between devices with their start and end apart: 19, of which 8 were waited for; matrix products, arithmetic and copies ran while one was open for 18% of the time, Pallas kernels for 9%

profile of v1, /device:TPU:0, one launch (start us, length us, event | category | flops | bytes accessed | tf_op | source)
XLA Modules:
  0.0 1015.6 jit_solution(9430202826526937599)
XLA Ops:
  9.4 62.9 %all-gather.10.cloned.1.call-done = bf16[3,768,384]{2,1,0:T(8,128)(2,1)} async-done(((bf16[3,48,384]{2,1,0:T(8,128)(2,1)}), bf16[3,768,384]{2,1,0:T(8,128)(2,1)}) %all-gather.10.cloned.1.call-update) | async-done | bytes 1769488 | tf_op jit(solution)/shard_map/all_gather | solution.py:343
  72.5 46.2 %all_gather.34 = bf16[768,384]{1,0:T(8,128)(2,1)} all-gather(bf16[48,384]{1,0:T(8,128)(2,1)} %bitcast.159), channel_id=1, replica_groups=mesh['shard'=4,'ctx'=4,'tp'=2] {'shard','ctx'}, dimensions={0}, use_global_device_ids=true | all-gather | bytes 626688 | tf_op jit(solution)/shard_map/all_gather | solution.py:343
  118.8 19.1 %all-gather.16.cloned.1.call-done = bf16[768,1536]{1,0:T(8,128)(2,1)} async-done(((bf16[48,1536]{1,0:T(8,128)(2,1)}), bf16[768,1536]{1,0:T(8,128)(2,1)}) %all-gather.16.cloned.1.call-update) | async-done | bytes 2359312 | tf_op jit(solution)/shard_map/all_gather | solution.py:343
  141.7 52.2 %all-gather.1 = bf16[16,13,48]{2,1,0:T(8,128)(2,1)S(1)} all-gather(bf16[1,13,48]{2,1,0:T(8,128)(2,1)S(1)} %bitcast.160), channel_id=2, replica_groups=mesh['shard'=4,'ctx'=4,'tp'=2] {'shard','ctx'}, dimensions={0}, use_global_device_ids=true | all-gather | bytes 21216 | tf_op jit(solution)/shard_map/all_gather | solution.py:364
  209.3 10.6 %all-to-all-done.2 = bf16[8,128,768]{2,1,0:T(8,128)(2,1)S(1)} async-done(((bf16[8,128,768]{2,1,0:T(8,128)(2,1)}), bf16[8,128,768]{2,1,0:T(8,128)(2,1)S(1)}, u32[]{:S(2)}, u32[]{:S(2)}) %all-to-all-start.2) | async-done | bytes 1572896 | tf_op jit(solution)/shard_map/all_to_all | solution.py:333
  225.6 45.8 %attend.1 = (bf16[1,1024,768]{2,1,0:T(8,128)(2,1)}, bf16[1,1024,768]{2,1,0:T(8,128)(2,1)}, bf16[1,1024,768]{2,1,0:T(8,128)(2,1)}, bf16[1,1024,768]{2,1,0:T(8,128)(2,1)}, f32[1,12,1024]{2,1,0:T(8,128)}) custom-call(s32[1,8]{1,0:T(1,128)} %get-tuple-element.142.first_ref, s32[1,8]{1,0:T(1,128)} %get-tuple-element.141.count_ref, ...), custom_call_target="tpu_custom_call" | custom-call | flops 6000000000 | bytes 12582912 | tf_op jit(solution)/shard_map/attend/pallas_call | solution.py:214
  277.2 50.3 %fusion.2 = (bf16[1024,3072]{1,0:T(8,128)(2,1)}, f32[1024,3072]{1,0:T(8,128)}) fusion(f32[3072]{0:T(1024)S(1)} %add.211, bf16[768,3072]{1,0:T(8,128)(2,1)} %all-gather.18.cloned.1.call-done, f32[1024,768]{0,1:T(8,128)} %copy-done.1, f32[768]{0:T(1024)S(1)} %add.208, f32[768]{0:T(1024)S(1)} %mul.231, f32[1024]{0:T(1024)S(1)} %add_rsqrt_fusion.1, ...), kind=kOutput, calls=%fused_computation.4 | convolution fusion | flops 5043388416 | bytes 26765312 | tf_op jit(solution)/shard_map/dot_general | solution.py:29
  327.5 9.3 fusion.54
  341.0 13.3 %convert_reduce_fusion = (f32[3072]{0:T(1024)S(1)}, bf16[1024,3072]{1,0:T(8,128)(2,1)S(1)}) fusion(f32[1024,3072]{1,0:T(8,128)} %get-tuple-element.146, f32[3072]{0:T(1024)S(1)} %add.211, bf16[768,3072]{1,0:T(8,128)(2,1)S(1)} %copy-done.19, f32[1024,768]{0,1:T(8,128)S(1)} %get-tuple-element.127), kind=kOutput, calls=%fused_computation.11 | convolution fusion | flops 4873516032 | bytes 26763264 | tf_op jit(solution)/shard_map/dot_general | solution.py:29
  354.3 5.9 multiply_reduce_fusion.1
  367.9 4.8 fusion.25.g_ref
  372.7 43.6 %attend_back.1 = bf16[1,1024,2304]{2,1,0:T(8,128)(2,1)} custom-call(s32[1,8]{1,0:T(1,128)} %get-tuple-element.142.first_ref, s32[1,8]{1,0:T(1,128)} %get-tuple-element.141.count_ref, bf16[1,1024,768]{2,1,0:T(8,128)(2,1)} %get-tuple-element.20.q_ref, bf16[1,1024,768]{2,1,0:T(8,128)(2,1)} %get-tuple-element.21.k_ref, ...), custom_call_target="tpu_custom_call" | custom-call | flops 12000000000 | bytes 14680064 | tf_op jit(solution)/shard_map/attend_back/pallas_call | solution.py:240
  425.2 9.8 convolution_convert_fusion.1
  437.0 9.4 convolution_convert_fusion
  448.8 5.4 copy.109
  455.2 12.8 %reduce-scatter.18.cloned.1.call-done = bf16[768,1536]{1,0:T(8,128)(2,1)} async-done(((bf16[768,3072]{1,0:T(8,128)(2,1)}), bf16[768,1536]{1,0:T(8,128)(2,1)}) %reduce-scatter.18.cloned.1.call-update) | async-done | bytes 2359312 | tf_op jit(solution)/shard_map/reduce_scatter | solution.py:417
  476.8 7.2 copy.108
  484.5 11.4 %reduce.42 = bf16[1024,768]{1,0:T(8,128)(2,1)} reduce(bf16[1024,1,768]{2,1,0:T(2,128)(2,1)S(1)} %bitcast.133, bf16[]{:T(256)} %broadcast.516), dimensions={1}, to_apply=%bitcast.112.reduce_sub_computation | reduce | bytes 3145730
  505.5 7.2 copy.101
  512.7 11.4 %reduce.41 = bf16[1024,768]{1,0:T(8,128)(2,1)} reduce(bf16[1024,1,768]{2,1,0:T(2,128)(2,1)S(1)} %bitcast.134, bf16[]{:T(256)} %broadcast.516), dimensions={1}, to_apply=%bitcast.110.reduce_sub_computation | reduce | bytes 3145730
  535.8 51.7 %psum.7 = f32[16,13,48]{2,0,1:T(8,128)S(1)} all-reduce(f32[16,13,48]{2,0,1:T(8,128)S(1)} %pad_maximum_fusion.1), channel_id=1, replica_groups=mesh['shard'=4,'ctx'=4,'tp'=2] {'shard','ctx','tp'}, use_global_device_ids=true, to_apply=%region_26.27 | all-reduce | flops 9984 | bytes 79872 | tf_op jit(solution)/shard_map/psum | solution.py:441
  606.5 135.2 %all-reduce.3.cloned.1.call-done = bf16[3,768,384]{2,0,1:T(4,128)(2,1)} async-done(((bf16[3,768,384]{2,0,1:T(4,128)(2,1)}), bf16[3,768,384]{2,0,1:T(4,128)(2,1)}) %all-reduce.3.cloned.1.call-update) | async-done | bytes 1769488
  743.3 130.8 %reduce-scatter.16.cloned.1.call-done = bf16[48,1536]{1,0:T(8,128)(2,1)} async-done(((bf16[768,1536]{1,0:T(8,128)(2,1)}), bf16[48,1536]{1,0:T(8,128)(2,1)}) %reduce-scatter.16.cloned.1.call-update) | async-done | bytes 147472 | tf_op jit(solution)/shard_map/reduce_scatter | solution.py:420
  875.8 131.5 %reduce-scatter.20.cloned.1.call-done = bf16[48,1536]{1,0:T(8,128)(2,1)} async-done(((bf16[768,1536]{1,0:T(8,128)(2,1)}), bf16[48,1536]{1,0:T(8,128)(2,1)}) %reduce-scatter.20.cloned.1.call-update) | async-done | bytes 147472 | tf_op jit(solution)/shard_map/reduce_scatter | solution.py:420
  (192 shorter events, 112.2 us)
Async XLA Ops:
  7.2 65.2 %all-gather.10.cloned.1.call-start = ((), (), s32[]{:S(2)}) async-start(), calls=%async_computation.11 | async-start | bytes 1880064 | tf_op jit(solution)/shard_map/all_gather | solution.py:343
  7.9 130.0 %all-gather.16.cloned.1.call-start = ((), (), s32[]{:S(2)}) async-start(), calls=%async_computation.14 | async-start | bytes 2506752 | tf_op jit(solution)/shard_map/all_gather | solution.py:343
  8.7 216.8 %all-gather.20.cloned.1.call-start = ((), (), s32[]{:S(2)}) async-start(), calls=%async_computation.16 | async-start | bytes 2506752 | tf_op jit(solution)/shard_map/all_gather | solution.py:343
  9.4 216.2 %all-gather.12.cloned.1.call-start = ((), (), s32[]{:S(2)}) async-start(), calls=%async_computation.12 | async-start | bytes 5308416 | tf_op jit(solution)/shard_map/all_gather | solution.py:344
  72.4 199.0 %all-gather.14.cloned.1.call-start = ((), (), s32[]{:S(2)}) async-start(), calls=%async_computation.13 | async-start | bytes 1769472 | tf_op jit(solution)/shard_map/all_gather | solution.py:344
  118.6 23.0 %copy-start.12 = (bf16[3,48]{1,0:T(4,128)(2,1)S(1)}, bf16[3,48]{1,0:T(4,128)(2,1)}, u32[]{:S(2)}) copy-start(bf16[3,48]{1,0:T(4,128)(2,1)} %param.21) | copy-start | bytes 868
  118.6 23.0 %copy-start.13 = (bf16[48]{0:T(256)(128)(2,1)S(1)}, bf16[48]{0:T(256)(128)(2,1)}, u32[]{:S(2)}) copy-start(bf16[48]{0:T(256)(128)(2,1)} %param.22) | copy-start | bytes 292
  118.6 23.0 %copy-start.14 = (bf16[48]{0:T(256)(128)(2,1)S(1)}, bf16[48]{0:T(256)(128)(2,1)}, u32[]{:S(2)}) copy-start(bf16[48]{0:T(256)(128)(2,1)} %param.24) | copy-start | bytes 292
  118.6 23.0 %copy-start.15 = (bf16[48]{0:T(256)(128)(2,1)S(1)}, bf16[48]{0:T(256)(128)(2,1)}, u32[]{:S(2)}) copy-start(bf16[48]{0:T(256)(128)(2,1)} %param.25) | copy-start | bytes 292
  118.6 23.0 %copy-start.16 = (bf16[48]{0:T(256)(128)(2,1)S(1)}, bf16[48]{0:T(256)(128)(2,1)}, u32[]{:S(2)}) copy-start(bf16[48]{0:T(256)(128)(2,1)} %param.26) | copy-start | bytes 292
  118.7 158.5 %all-gather.18.cloned.1.call-start = ((), (), s32[]{:S(2)}) async-start(), calls=%async_computation.15 | async-start | bytes 7077888 | tf_op jit(solution)/shard_map/all_gather | solution.py:344
  137.9 57.5 %all-to-all-start = ((bf16[8,128,768]{2,1,0:T(8,128)(2,1)}), bf16[8,128,768]{2,1,0:T(8,128)(2,1)S(1)}, u32[]{:S(2)}, u32[]{:S(2)}) async-start(bf16[8,128,768]{2,1,0:T(8,128)(2,1)} %param.16), calls=%async_computation | async-start | bytes 3145728 | tf_op jit(solution)/shard_map/all_to_all | solution.py:333
  195.4 24.6 %all-to-all-start.2 = ((bf16[8,128,768]{2,1,0:T(8,128)(2,1)}), bf16[8,128,768]{2,1,0:T(8,128)(2,1)S(1)}, u32[]{:S(2)}, u32[]{:S(2)}) async-start(bf16[8,128,768]{2,1,0:T(8,128)(2,1)} %param.31), calls=%async_computation.2 | async-start | bytes 3145728 | tf_op jit(solution)/shard_map/all_to_all | solution.py:333
  199.0 128.6 %all-gather.22.cloned.1.call-start = ((), (), s32[]{:S(2)}) async-start(), calls=%async_computation.17 | async-start | bytes 7077888 | tf_op jit(solution)/shard_map/all_gather | solution.py:344
  225.5 221.0 %reduce-scatter.22.cloned.1.call-start = ((), (), s32[]{:S(2)}) async-start(), calls=%async_computation.24 | async-start | bytes 1769472
  367.9 80.9 %reduce-scatter.10.cloned.1.call-start = ((), (), s32[]{:S(2)}) async-start(), calls=%async_computation.18 | async-start | bytes 5308416 | tf_op jit(solution)/shard_map/reduce_scatter | solution.py:417
  425.1 29.1 %reduce-scatter.14.cloned.1.call-start = ((), (), s32[]{:S(2)}) async-start(), calls=%async_computation.20 | async-start | bytes 7077888 | tf_op jit(solution)/shard_map/reduce_scatter | solution.py:417
  435.0 33.0 %reduce-scatter.18.cloned.1.call-start = ((), (), s32[]{:S(2)}) async-start(), calls=%async_computation.22 | async-start | bytes 7077888 | tf_op jit(solution)/shard_map/reduce_scatter | solution.py:417
  446.4 158.7 %reduce-scatter.12.cloned.1.call-start = ((), (), s32[]{:S(2)}) async-start(), calls=%async_computation.19 | async-start | bytes 626688 | tf_op jit(solution)/shard_map/reduce_scatter | solution.py:420
  448.7 293.0 %all-reduce.3.cloned.1.call-start = ((), (), s32[]{:S(2)}) async-start(), calls=%async_computation.25 | async-start | bytes 4718592
  454.2 420.0 %reduce-scatter.16.cloned.1.call-start = ((), (), s32[]{:S(2)}) async-start(), calls=%async_computation.21 | async-start | bytes 2506752 | tf_op jit(solution)/shard_map/reduce_scatter | solution.py:420
  454.8 552.5 %reduce-scatter.20.cloned.1.call-start = ((), (), s32[]{:S(2)}) async-start(), calls=%async_computation.23 | async-start | bytes 2506752 | tf_op jit(solution)/shard_map/reduce_scatter | solution.py:420
  499.7 28.1 %all-to-all-start.3 = ((bf16[8,2,49152]{2,1,0:T(2,128)(2,1)}), bf16[8,2,49152]{2,1,0:T(2,128)(2,1)}, u32[]{:S(2)}, u32[]{:S(2)}) async-start(bf16[8,2,49152]{2,1,0:T(2,128)(2,1)} %reshape.571), calls=%async_computation.3 | async-start | bytes 3145728 | tf_op jit(solution)/shard_map/all_to_all | solution.py:336
  527.8 67.6 %all-to-all-start.1 = ((bf16[8,2,49152]{2,1,0:T(2,128)(2,1)}), bf16[8,2,49152]{2,1,0:T(2,128)(2,1)}, u32[]{:S(2)}, u32[]{:S(2)}) async-start(bf16[8,2,49152]{2,1,0:T(2,128)(2,1)} %reshape.569), calls=%async_computation.1 | async-start | bytes 3145728 | tf_op jit(solution)/shard_map/all_to_all | solution.py:336
  (23 other events, 194.7 us)
Sparse Core Ops, SparseCore 0:
  10.7 61.6 all-gather.9
  75.2 62.6 all-gather.15
  140.7 66.0 all-gather.19
  208.1 15.0 all-gather.11
  224.6 10.3 all-gather.13
  236.4 15.6 all-gather.17
  253.6 15.6 all-gather.21
  368.0 7.6 reduce-scatter.21
  425.3 10.5 reduce-scatter.9
  438.0 13.7 reduce-scatter.13
  454.2 13.7 reduce-scatter.17
  472.5 132.4 reduce-scatter.11
  611.6 130.0 all-reduce.2
  746.4 127.6 reduce-scatter.15
  879.7 127.5 reduce-scatter.19

commit v2 on v1

--- a/solution.py
+++ b/solution.py
@@ -285,6 +285,395 @@
     return jnp.cos(phase), jnp.sin(phase)
 
 
+MESH = pl.DeviceIdType.MESH
+ROWS = ("shard", "ctx")
+EVERY = ("shard", "ctx", "tp")
+SEQ = ("ctx", "tp")
+
+ROUTES = {"up": "zyx", "attend": "zyx", "down": "zxy", "project": "xyz", "vectors": "xyz"}
+ITEMS = ("project", "up", "down", "attend", "vectors")
+
+
+def places(depth):
+    steps = [0]
+    for k in range(1, depth):
+        steps += [k, -k]
+    return [(k, dy, dx) for k in steps for dy in (0, 1) for dx in (0, 1)]
+
+
+def hops(place):
+    return abs(place[0]) + place[1] + place[2]
+
+
+def links(route, place, depth):
+    apart = {"z": place[0] != 0, "y": place[1], "x": place[2]}
+    level = max([i for i, axis in enumerate(route) if apart[axis]], default=-1)
+    sign = (place[0] > 0) - (place[0] < 0)
+    onward = []
+    if level >= 0 and route[level] == "z" and abs(place[0]) + 1 < depth:
+        onward.append(("z", -sign))
+    for axis in route[level + 1 :]:
+        onward += [("z", 1), ("z", -1)] if axis == "z" else [(axis, 1)]
+    back = None if level < 0 else (route[level], sign if route[level] == "z" else 1)
+    return back, onward
+
+
+def seen_from(place, link):
+    k, dy, dx = place
+    axis, way = link
+    return {"z": (k - way, dy, dx), "y": (k, 1 - dy, dx), "x": (k, dy, 1 - dx)}[axis]
+
+
+class Here:
+    def __init__(self):
+        self.depth = lax.axis_size("shard")
+        self.z = lax.axis_index("shard")
+        self.c = lax.axis_index("ctx")
+        self.t = lax.axis_index("tp")
+        self.y = self.c // 2
+        self.x = self.c % 2
+
+    def device(self, link):
+        axis, way = link
+        if axis == "z":
+            return (self.z + way, self.c, self.t)
+        if axis == "y":
+            return (self.z, 2 * (1 - self.y) + self.x, self.t)
+        if axis == "x":
+            return (self.z, 2 * self.y + (1 - self.x), self.t)
+        return (self.z, self.c, 1 - self.t)
+
+    def piece(self, place):
+        k, dy, dx = place
+        y = 1 - self.y if dy else self.y
+        x = 1 - self.x if dx else self.x
+        return (self.z + k) * 4 + 2 * y + x
+
+    def inside(self, way):
+        if way == 0:
+            return None
+        return self.z + way < self.depth if way > 0 else self.z + way >= 0
+
+    def meet(self):
+        barrier = pltpu.get_barrier_semaphore()
+        for link in (("x", 1), ("y", 1), ("tp", 1)):
+            pl.semaphore_signal(barrier, inc=1, device_id=self.device(link), device_id_type=MESH)
+        for way in (1, -1):
+
+            @pl.when(self.inside(way))
+            def _():
+                pl.semaphore_signal(
+                    barrier, inc=1, device_id=self.device(("z", way)), device_id_type=MESH
+                )
+
+        peers = 3 + (self.z > 0).astype(jnp.int32) + (self.z < self.depth - 1).astype(jnp.int32)
+        pl.semaphore_wait(barrier, peers)
+
+
+def guarded(condition, action):
+    if condition is None:
+        action()
+    else:
+        pl.when(condition)(action)
+
+
+def columns(half, width):
+    return pl.ds(pl.multiple_of(half * width, LANES), width)
+
+
+def block_of(name, ref, piece, half, width):
+    if name == "project":
+        return ref.at[:, piece, :, columns(half, width)]
+    if name == "vectors":
+        return ref.at[piece]
+    return ref.at[piece, :, columns(half, width)]
+
+
+def gather_kernel(widths, chip_count, *refs):
+    count = len(ITEMS)
+    shards = dict(zip(ITEMS, refs[:count]))
+    wholes = dict(zip(ITEMS, refs[count : 2 * count]))
+    send_sem, recv_sem, side_send, side_recv, own_sem = refs[2 * count :]
+    here = Here()
+    spots = places(chip_count)
+    order = sorted(spots, key=hops)
+    slot = {}
+    for i, name in enumerate(ITEMS):
+        for place in spots:
+            for link in links(ROUTES[name], place, chip_count)[1]:
+                slot[name, place, link] = len(slot)
+
+    def block(name, place, half):
+        return block_of(name, wholes[name], here.piece(place), half, widths[name])
+
+    def send(name, place, link):
+        source = shards[name] if place == (0, 0, 0) else block(name, place, here.t)
+        return pltpu.make_async_remote_copy(
+            src_ref=source,
+            dst_ref=block(name, place, here.t),
+            send_sem=send_sem.at[slot[name, place, link]],
+            recv_sem=recv_sem.at[ITEMS.index(name), spots.index(seen_from(place, link))],
+            device_id=here.device(link),
+            device_id_type=MESH,
+        )
+
+    def side(name, place, half):
+        source = shards[name] if place == (0, 0, 0) else block(name, place, half)
+        return pltpu.make_async_remote_copy(
+            src_ref=source,
+            dst_ref=block(name, place, half),
+            send_sem=side_send.at[ITEMS.index(name), spots.index(place)],
+            recv_sem=side_recv.at[ITEMS.index(name), spots.index(place)],
+            device_id=here.device(("tp", 1)),
+            device_id_type=MESH,
+        )
+
+    def arrival(name, place):
+        return pltpu.make_async_remote_copy(
+            src_ref=block(name, place, here.t),
+            dst_ref=block(name, place, here.t),
+            send_sem=send_sem.at[0],
+            recv_sem=recv_sem.at[ITEMS.index(name), spots.index(place)],
+            device_id=here.device(("tp", 1)),
+            device_id_type=MESH,
+        )
+
+    here.meet()
+    for name in ITEMS:
+        pltpu.make_async_copy(
+            shards[name], block(name, (0, 0, 0), here.t), own_sem.at[ITEMS.index(name)]
+        ).start()
+    for place in order:
+
+        def pass_on(place=place):
+            for name in ITEMS:
+                if place != (0, 0, 0):
+                    arrival(name, place).wait_recv()
+                for link in links(ROUTES[name], place, chip_count)[1]:
+                    guarded(
+                        here.inside(link[1]) if link[0] == "z" else None,
+                        lambda link=link: send(name, place, link).start(),
+                    )
+                if name != "vectors":
+                    side(name, place, here.t).start()
+
+        guarded(here.inside(place[0]), pass_on)
+    for place in order:
+
+        def finish(place=place):
+            for name in ITEMS:
+                if name != "vectors":
+                    side(name, place, 1 - here.t).wait_recv()
+                    side(name, place, here.t).wait_send()
+                for link in links(ROUTES[name], place, chip_count)[1]:
+                    guarded(
+                        here.inside(link[1]) if link[0] == "z" else None,
+                        lambda link=link: send(name, place, link).wait_send(),
+                    )
+
+        guarded(here.inside(place[0]), finish)
+    for name in ITEMS:
+        pltpu.make_async_copy(
+            shards[name], block(name, (0, 0, 0), here.t), own_sem.at[ITEMS.index(name)]
+        ).wait()
+
+
+def link_count(depth):
+    return sum(len(links(ROUTES[name], place, depth)[1]) for name in ITEMS for place in places(depth))
+
+
+def gather_weights(shards):
+    chips, pieces = lax.axis_size("shard"), lax.axis_size("shard") * lax.axis_size("ctx")
+    widths = {name: shards[name].shape[-1] for name in ITEMS}
+    shapes = []
+    for name in ITEMS:
+        shape = shards[name].shape
+        if name == "project":
+            shape = (shape[0], pieces, shape[1], 2 * shape[2])
+        elif name == "vectors":
+            shape = (pieces,) + shape
+        else:
+            shape = (pieces, shape[0], 2 * shape[1])
+        shapes.append(jax.ShapeDtypeStruct(shape, jnp.bfloat16))
+    spots = len(places(chips))
+    outs = pl.pallas_call(
+        lambda *refs: gather_kernel(widths, chips, *refs),
+        out_shape=shapes,
+        in_specs=[pl.BlockSpec(memory_space=pl.ANY)] * len(ITEMS),
+        out_specs=[pl.BlockSpec(memory_space=pl.ANY)] * len(ITEMS),
+        scratch_shapes=[
+            pltpu.SemaphoreType.DMA((link_count(chips),)),
+            pltpu.SemaphoreType.DMA((len(ITEMS), spots)),
+            pltpu.SemaphoreType.DMA((len(ITEMS), spots)),
+            pltpu.SemaphoreType.DMA((len(ITEMS), spots)),
+            pltpu.SemaphoreType.DMA((len(ITEMS),)),
+        ],
+        compiler_params=pltpu.CompilerParams(collective_id=0, has_side_effects=True),
+        name="gather_weights",
+    )(*[shards[name] for name in ITEMS])
+    return dict(zip(ITEMS, outs))
+
+
+def add_into(target, addend):
+    lead = target.shape[:-2]
+    for index in range(math.prod(lead)):
+        at = (index,) if lead else ()
+        height = 16 if target.shape[-2] % 16 == 0 else 8
+
+        @pl.loop(0, target.shape[-2] // height)
+        def _(step):
+            rows = pl.ds(pl.multiple_of(step * height, height), height)
+            where = at + (rows, slice(None))
+            total = target[where].astype(jnp.float32) + addend[where].astype(jnp.float32)
+            target[where] = total.astype(target.dtype)
+
+
+def scatter_kernel(widths, chip_count, *refs):
+    count = len(ITEMS)
+    grads = dict(zip(ITEMS, refs[:count]))
+    outs = dict(zip(ITEMS, refs[count : 2 * count]))
+    mine = dict(zip(ITEMS, refs[2 * count : 3 * count]))
+    theirs = dict(zip(ITEMS, refs[3 * count : 4 * count]))
+    inbox = dict(zip(ITEMS, refs[4 * count : 5 * count]))
+    load_sem, side_send, side_recv, send_sem, recv_sem = refs[5 * count :]
+    here = Here()
+    spots = places(chip_count)
+    order = sorted(spots, key=hops, reverse=True)
+    slot = {}
+    box = {}
+    for name in ITEMS:
+        local = 0
+        for place in spots:
+            for link in links(ROUTES[name], place, chip_count)[1]:
+                slot[name, place, link] = len(slot)
+                box[name, place, link] = local
+                local += 1
+
+    def opposite(link):
+        return (link[0], -link[1]) if link[0] == "z" else link
+
+    def load(name, place):
+        return pltpu.make_async_copy(
+            block_of(name, grads[name], here.piece(place), here.t, widths[name]),
+            mine[name].at[spots.index(place)],
+            load_sem.at[ITEMS.index(name), spots.index(place)],
+        )
+
+    def side(name, place):
+        return pltpu.make_async_remote_copy(
+            src_ref=block_of(name, grads[name], here.piece(place), 1 - here.t, widths[name]),
+            dst_ref=theirs[name].at[spots.index(place)],
+            send_sem=side_send.at[ITEMS.index(name), spots.index(place)],
+            recv_sem=side_recv.at[ITEMS.index(name), spots.index(place)],
+            device_id=here.device(("tp", 1)),
+            device_id_type=MESH,
+        )
+
+    def send(name, place, link):
+        there = seen_from(place, link)
+        return pltpu.make_async_remote_copy(
+            src_ref=mine[name].at[spots.index(place)],
+            dst_ref=inbox[name].at[box[name, there, opposite(link)]],
+            send_sem=send_sem.at[ITEMS.index(name), spots.index(place)],
+            recv_sem=recv_sem.at[slot[name, there, opposite(link)]],
+            device_id=here.device(link),
+            device_id_type=MESH,
+        )
+
+    def arrival(name, place, link):
+        return pltpu.make_async_remote_copy(
+            src_ref=inbox[name].at[box[name, place, link]],
+            dst_ref=inbox[name].at[box[name, place, link]],
+            send_sem=send_sem.at[0, 0],
+            recv_sem=recv_sem.at[slot[name, place, link]],
+            device_id=here.device(link),
+            device_id_type=MESH,
+        )
+
+    here.meet()
+    for place in order:
+
+        def begin(place=place):
+            for name in ITEMS:
+                side(name, place).start()
+                load(name, place).start()
+
+        guarded(here.inside(place[0]), begin)
+    for place in order:
+
+        def settle(place=place):
+            for name in ITEMS:
+                back, onward = links(ROUTES[name], place, chip_count)
+                total = mine[name].at[spots.index(place)]
+                load(name, place).wait()
+                side(name, place).wait_recv()
+                add_into(total, theirs[name].at[spots.index(place)])
+                for link in onward:
+
+                    def take(link=link):
+                        arrival(name, place, link).wait_recv()
+                        add_into(total, inbox[name].at[box[name, place, link]])
+
+                    guarded(here.inside(link[1]) if link[0] == "z" else None, take)
+                if back is not None:
+                    send(name, place, back).start()
+
+        guarded(here.inside(place[0]), settle)
+    for name in ITEMS:
+        outs[name][...] = mine[name][spots.index((0, 0, 0))].astype(jnp.float32)
+    for place in order:
+
+        def finish(place=place):
+            for name in ITEMS:
+                back, _ = links(ROUTES[name], place, chip_count)
+                side(name, place).wait_send()
+                if back is not None:
+                    send(name, place, back).wait_send()
+
+        guarded(here.inside(place[0]), finish)
+
+
+def scatter_grads(grads):
+    chips = lax.axis_size("shard")
+    spots = len(places(chips))
+    widths, blocks, boxes = {}, [], []
+    for name in ITEMS:
+        shape = grads[name].shape
+        if name == "project":
+            block = (shape[0], shape[2], shape[3] // 2)
+        elif name == "vectors":
+            block = shape[1:]
+        else:
+            block = (shape[1], shape[2] // 2)
+        widths[name] = block[-1]
+        blocks.append(block)
+        boxes.append(sum(len(links(ROUTES[name], place, chips)[1]) for place in places(chips)))
+    kinds = [grads[name].dtype for name in ITEMS]
+    outs = pl.pallas_call(
+        lambda *refs: scatter_kernel(widths, chips, *refs),
+        out_shape=[jax.ShapeDtypeStruct(block, jnp.float32) for block in blocks],
+        in_specs=[pl.BlockSpec(memory_space=pl.ANY)] * len(ITEMS),
+        out_specs=[pl.BlockSpec(memory_space=pltpu.VMEM)] * len(ITEMS),
+        scratch_shapes=(
+            [pltpu.VMEM((spots,) + block, kind) for block, kind in zip(blocks, kinds)]
+            + [pltpu.VMEM((spots,) + block, kind) for block, kind in zip(blocks, kinds)]
+            + [pltpu.VMEM((box,) + block, kind) for box, block, kind in zip(boxes, blocks, kinds)]
+            + [
+                pltpu.SemaphoreType.DMA((len(ITEMS), spots)),
+                pltpu.SemaphoreType.DMA((len(ITEMS), spots)),
+                pltpu.SemaphoreType.DMA((len(ITEMS), spots)),
+                pltpu.SemaphoreType.DMA((len(ITEMS), spots)),
+                pltpu.SemaphoreType.DMA((link_count(chips),)),
+            ]
+        ),
+        compiler_params=pltpu.CompilerParams(
+            collective_id=1, has_side_effects=True, vmem_limit_bytes=60 << 20
+        ),
+        name="scatter_grads",
+    )(*[grads[name] for name in ITEMS])
+    return dict(zip(ITEMS, outs))
+
+
 def normalize(rows, gain, shift):
     mean = jnp.mean(rows, axis=-1, keepdims=True)
     centred = rows - mean
@@ -311,9 +700,33 @@
     return cumulative + values * density
 
 
-ROWS = ("shard", "ctx")
-EVERY = ("shard", "ctx", "tp")
-SEQ = ("ctx", "tp")
+def fitting(shards):
+    return lax.axis_size("ctx") == 4 and lax.axis_size("tp") == 2 and shards["up"].shape[0] % 16 == 0
+
+
+def gather_plain(shards):
+    wholes = {}
+    for name in ITEMS:
+        axis = 1 if name == "project" else 0
+        part = lax.all_gather(shards[name], ROWS, axis=axis)
+        if name != "vectors":
+            part = lax.all_gather(part, "tp", axis=axis + 2, tiled=True)
+        wholes[name] = part
+    return wholes
+
+
+def scatter_plain(grads):
+    shards = {}
+    for name in ITEMS:
+        axis = 1 if name == "project" else 0
+        part = grads[name]
+        if name == "vectors":
+            part = lax.psum(part, "tp")
+        else:
+            part = lax.psum_scatter(part, "tp", scatter_dimension=axis + 2, tiled=True)
+        part = lax.psum_scatter(part, ROWS, scatter_dimension=axis, tiled=False)
+        shards[name] = part.astype(jnp.float32)
+    return shards
 
 
 def local(
@@ -330,23 +743,17 @@
     depth = D // pieces
 
     def to_sequences(array):
-        return lax.all_to_all(array, SEQ, 0, 1, tiled=True)
+        parts = array.reshape((members, own) + array.shape[1:])
+        parts = lax.all_to_all(parts, SEQ, 0, 0, tiled=True)
+        return jnp.swapaxes(parts, 0, 1).reshape(own, S, D)
 
     def to_blocks(array):
-        return lax.all_to_all(array, SEQ, 1, 0, tiled=True)
+        parts = jnp.swapaxes(array.reshape(own, members, S // members, D), 0, 1)
+        return lax.all_to_all(parts, SEQ, 0, 0, tiled=True).reshape(tokens.shape)
 
     x = to_sequences(tokens)
     segments = lax.dynamic_slice_in_dim(segment_ids, rank * own, own, 0)
     pads = lax.dynamic_slice_in_dim(padding, rank * own, own, 0)
-
-    def gather(shard, axis):
-        part = lax.all_gather(shard, ROWS, axis=axis, tiled=True)
-        return lax.all_gather(part, "tp", axis=axis + 1, tiled=True)
-
-    project = gather(jnp.transpose(project_weight, (1, 0, 2)), 1)
-    attend_t = gather(jnp.transpose(attend_weight), 0)
-    up = gather(up_weight, 0)
-    down_t = gather(jnp.transpose(down_weight), 0)
 
     vectors = jnp.concatenate(
         [
@@ -361,7 +768,20 @@
         ],
         axis=0,
     )
-    vectors = lax.all_gather(vectors, ROWS, axis=0).astype(jnp.float32)
+    shards = {
+        "project": jnp.transpose(project_weight, (1, 0, 2)),
+        "up": up_weight,
+        "down": jnp.transpose(down_weight),
+        "attend": jnp.transpose(attend_weight),
+        "vectors": jnp.pad(vectors, ((0, 3), (0, LANES - depth))),
+    }
+    custom = fitting(shards)
+    wholes = gather_weights(shards) if custom else gather_plain(shards)
+    project = wholes["project"].reshape(3, D, D)
+    up = wholes["up"].reshape(D, FF)
+    down_t = wholes["down"].reshape(D, FF)
+    attend_t = wholes["attend"].reshape(D, D)
+    vectors = wholes["vectors"][:, :13, :depth].astype(jnp.float32)
     wide = jnp.transpose(vectors[:, :9], (1, 0, 2)).reshape(9, D)
     up_shift = vectors[:, 9:].reshape(FF)
 
@@ -412,12 +832,6 @@
         dot(joint_grad[:, i * D : (i + 1) * D], project[i], NT) for i in range(3)
     )
     tokens_grad = to_blocks((first_grad + token_part).astype(jnp.bfloat16).reshape(own, S, D))
-
-    def scatter(grad, axis):
-        part = lax.psum_scatter(
-            grad.astype(jnp.bfloat16), "tp", scatter_dimension=axis + 1, tiled=True
-        )
-        return lax.psum_scatter(part, ROWS, scatter_dimension=axis, tiled=True).astype(jnp.float32)
 
     sums = jnp.concatenate(
         [
@@ -438,16 +852,22 @@
         ],
         axis=1,
     )
-    sums = lax.psum(sums, EVERY)
-    mine = lax.axis_index("shard") * lax.axis_size("ctx") + lax.axis_index("ctx")
-    sums = lax.dynamic_index_in_dim(sums, mine, 0, keepdims=False)
+    grads = {
+        "project": project_grad.astype(jnp.bfloat16).reshape(3, pieces, depth, D),
+        "up": up_grad.astype(jnp.bfloat16).reshape(pieces, depth, FF),
+        "down": down_t_grad.astype(jnp.bfloat16).reshape(pieces, depth, FF),
+        "attend": attend_t_grad.astype(jnp.bfloat16).reshape(pieces, depth, D),
+        "vectors": jnp.pad(sums, ((0, 0), (0, 3), (0, LANES - depth))),
+    }
+    shards = scatter_grads(grads) if custom else scatter_plain(grads)
+    sums = shards["vectors"][:13, :depth]
     return (
         output,
         tokens_grad,
-        jnp.transpose(scatter(project_grad, 1), (1, 0, 2)),
-        jnp.transpose(scatter(attend_t_grad, 0)),
-        scatter(up_grad, 0),
-        jnp.transpose(scatter(down_t_grad, 0)),
+        jnp.transpose(shards["project"], (1, 0, 2)),
+        jnp.transpose(shards["attend"]),
+        shards["up"],
+        jnp.transpose(shards["down"]),
         sums[:3],
         sums[3],
         sums[9:].reshape(-1),

time: 1020 us -> 426 us (0.42)
  waiting for transfers between devices: 509 us -> 6.92 us
  Pallas kernels: 89.5 us -> 240 us
  blocking collectives: 150 us -> 0 us
  local copies, waits for them, and re-layouts: 62.6 us -> 19.3 us
  other arithmetic: 48.9 us -> 25.9 us
  matrix products: 123 us -> 107 us
  between operations: 15.4 us -> 1.52 us
    reduce_scatter x6 -> x0, waiting for transfers between devices: 279 us -> none  [the longest x3 266 us: scatter(): lax.psum_scatter(part, ROWS, scatter_dimension=axis, tiled=True)]
    pallas_call x0 -> x2, Pallas kernels: none -> 150 us  [the longest x1 81 us: gather_weights(): pl.pallas_call(lambda *refs: gather_kernel(widths, chips, *refs), out_sha...]
    unnamed x17 -> x0, waiting for transfers between devices: 138 us -> none
    all_gather x2 -> x0, blocking collectives: 98.4 us -> none  [the longest x1 52.2 us: local(): vectors = lax.all_gather(vectors, ROWS, axis=0).astype(jnp.float32)]
    all_gather x7 -> x0, waiting for transfers between devices: 82.1 us -> none  [the longest x3 82.1 us: gather(): part = lax.all_gather(shard, ROWS, axis=axis, tiled=True)]
    psum x1 -> x0, blocking collectives: 51.7 us -> none  [local(): sums = lax.psum(sums, EVERY)]
    unnamed x74, local copies, waits for them, and re-layouts: 34.8 us -> 7.34 us
    unnamed x4 -> x3, other arithmetic: 22.8 us -> 0.01 us
  transfers between devices with their start and end apart: 19 -> 4, of which waited for: 8 -> 1; matrix products, arithmetic and copies ran while one was open for 18% -> 21% of each run, Pallas kernels for 9% -> 47%
where the time goes in v2:
time: 426 us; the launch traced here: 418 us
  Pallas kernels  240 us (56%)
  matrix products  107 us (25%)
  other arithmetic  25.9 us (6%)
  local copies, waits for them, and re-layouts  19.3 us (5%)
  starting transfers between devices  17.7 us (4%)
  waiting for transfers between devices  6.92 us (2%)
    dot_general x15, matrix products, dot(): lax.dot_general(left, right, dims, preferred_element_type=jnp.float32)  107 us
    pallas_call x1, Pallas kernels, gather_weights(): pl.pallas_call(lambda *refs: gather_kernel(widths, chips, *refs), out_sha...  81 us
    pallas_call x1, Pallas kernels, scatter_grads(): pl.pallas_call(lambda *refs: scatter_kernel(widths, chips, *refs), out_sh...  69.1 us
    pallas_call x1, Pallas kernels, attend(): pl.pallas_call(attend_kernel, grid_spec=pltpu.PrefetchScalarGridSpec(num_...  46 us
    pallas_call x1, Pallas kernels, attend_back(): pl.pallas_call(attend_back_kernel, grid_spec=pltpu.PrefetchScalarGridSpec...  43.4 us
    all_to_all x2, starting transfers between devices, to_sequences(): parts = lax.all_to_all(parts, SEQ, 0, 0, tiled=True)  9.6 us
  transfers between devices with their start and end apart: 4, of which 1 were waited for; matrix products, arithmetic and copies ran while one was open for 21% of the time, Pallas kernels for 47%

profile of v2, /device:TPU:0, one launch (start us, length us, event | category | flops | bytes accessed | tf_op | source)
XLA Modules:
  0.0 418.1 jit_solution(8519028597388785954)
XLA Ops:
  0.7 5.3 %all-to-all-start = ((bf16[8,1,128,768]{3,2,1,0:T(8,128)(2,1)}), bf16[8,1,128,768]{3,2,1,0:T(8,128)(2,1)S(1)}, u32[]{:S(2)}, u32[]{:S(2)}) async-start(bf16[8,1,128,768]{3,2,1,0:T(8,128)(2,1)} %bitcast.150), calls=%async_computation | async-start | bytes 3145728 | tf_op jit(solution)/shard_map/all_to_all | solution.py:747
  6.9 81.0 %gather_weights.1 = (bf16[3,16,48,768]{3,2,1,0:T(8,128)(2,1)}, bf16[16,48,3072]{2,1,0:T(8,128)(2,1)}, bf16[16,48,3072]{2,1,0:T(8,128)(2,1)}, bf16[16,48,768]{2,1,0:T(8,128)(2,1)}, bf16[16,16,128]{2,1,0:T(8,128)(2,1)}) custom-call(bf16[3,48,384]{2,1,0:T(8,128)(2,1)} %bitcast.168, bf16[48,1536]{1,0:T(8,128)(2,1)} %refs_1_.1, bf16[48,1536]{1,0:T(8,128)(2,1)} %bitcast.165, ...), custom_call_target="tpu_custom_call" | custom-call | tf_op jit(solution)/shard_map/gather_weights/pallas_call | solution.py:499
  95.7 3.0 multiply_sine_fusion
  98.7 3.8 fusion.49
  102.6 4.3 %all-to-all-start.2 = ((bf16[8,1,128,768]{3,2,1,0:T(8,128)(2,1)}), bf16[8,1,128,768]{3,2,1,0:T(8,128)(2,1)}, u32[]{:S(2)}, u32[]{:S(2)}) async-start(bf16[8,1,128,768]{3,2,1,0:T(8,128)(2,1)} %bitcast.28), calls=%async_computation.2 | async-start | bytes 3145728 | tf_op jit(solution)/shard_map/all_to_all | solution.py:747
  106.9 46.0 %attend.1 = (bf16[1,1024,768]{2,1,0:T(8,128)(2,1)}, bf16[1,1024,768]{2,1,0:T(8,128)(2,1)}, bf16[1,1024,768]{2,1,0:T(8,128)(2,1)}, bf16[1,1024,768]{2,1,0:T(8,128)(2,1)}, f32[1,12,1024]{2,1,0:T(8,128)}) custom-call(s32[1,8]{1,0:T(1,128)} %get-tuple-element.81.first_ref, s32[1,8]{1,0:T(1,128)} %get-tuple-element.80.count_ref, bf16[1,1024,768]{2,1,0:T(8,128)(2,1)} %bitcast.151, ...), custom_call_target="tpu_custom_call" | custom-call | flops 6000000000 | bytes 12582912 | tf_op jit(solution)/shard_map/attend/pallas_call | solution.py:214
  153.0 3.6 fusion.50
  157.1 34.6 %fusion.2 = (bf16[1024,3072]{1,0:T(8,128)(2,1)S(1)}, f32[1024,3072]{1,0:T(8,128)}) fusion(f32[3072]{0:T(1024)S(1)} %add.190, bf16[768,3072]{1,0:T(8,128)(2,1)S(1)} %bitcast.179, f32[1024,768]{1,0:T(8,128)S(1)} %get-tuple-element.83, f32[768]{0:T(1024)S(1)} %add.187, f32[768]{0:T(1024)S(1)} %mul.227, f32[1024]{0:T(1024)S(1)} %add_rsqrt_fusion.1, ...), kind=kOutput, calls=%fused_computation.4 | convolution fusion | flops 5043388416 | bytes 26765312 | tf_op jit(solution)/shard_map/dot_general | solution.py:29
  191.8 5.5 %fusion.51 = (f32[1024]{0:T(1024)S(1)}, f32[1024,768]{1,0:T(8,128)S(1)}) fusion(f32[768]{0:T(1024)S(1)} %add.193, bf16[1024,3072]{1,0:T(8,128)(2,1)S(1)} %get-tuple-element.84, bf16[768,3072]{1,0:T(8,128)(2,1)S(1)} %bitcast.186, f32[768]{0:T(1024)S(1)} %add.187, f32[768]{0:T(1024)S(1)} %mul.227, f32[1024]{0:T(1024)S(1)} %add_rsqrt_fusion.1, ...), kind=kOutput, calls=%fused_computation.137 | convolution fusion | flops 4837342208 | bytes 17323008 | tf_op jit(solution)/shard_map/dot_general | solution.py:29
  202.5 3.6 convert_reduce_fusion.3
  206.1 13.4 %convert_reduce_fusion = (f32[3072]{0:T(1024)S(1)}, bf16[1024,3072]{1,0:T(8,128)(2,1)S(1)}) fusion(f32[1024,3072]{1,0:T(8,128)} %get-tuple-element.85, f32[3072]{0:T(1024)S(1)} %add.190, bf16[768,3072]{1,0:T(8,128)(2,1)} %bitcast.183, f32[1024,768]{1,0:T(8,128)S(1)} %get-tuple-element.63), kind=kOutput, calls=%fused_computation.11 | convolution fusion | flops 4873516032 | bytes 26763264 | tf_op jit(solution)/shard_map/dot_general | solution.py:29
  219.6 6.0 %multiply_reduce_fusion = (f32[768]{0:T(1024)S(1)}, f32[1024]{0:T(1024)S(1)}, f32[1024]{0:T(1024)S(1)}, f32[768]{0:T(1024)S(1)}, f32[1024,768]{1,0:T(8,128)S(1)}) fusion(f32[1024,768]{1,0:T(8,128)S(1)} %copy-done.1, f32[1024]{0:T(1024)S(1)} %add_rsqrt_fusion.1, f32[1024]{0:T(1024)S(1)} %broadcast_multiply_fusion.4, f32[768]{0:T(1024)S(1)} %mul.227, ...), kind=kOutput, calls=%fused_computation.42 | convolution fusion | flops 4839698432 | bytes 20472832 | tf_op jit(solution)/shard_map/dot_general | solution.py:29
  229.4 43.4 %attend_back.1 = bf16[1,1024,2304]{2,1,0:T(8,128)(2,1)} custom-call(s32[1,8]{1,0:T(1,128)} %get-tuple-element.81.first_ref, s32[1,8]{1,0:T(1,128)} %get-tuple-element.80.count_ref, bf16[1,1024,768]{2,1,0:T(8,128)(2,1)} %get-tuple-element.35.q_ref, bf16[1,1024,768]{2,1,0:T(8,128)(2,1)} %get-tuple-element.36.k_ref, ...), custom_call_target="tpu_custom_call" | custom-call | flops 12000000000 | bytes 14680064 | tf_op jit(solution)/shard_map/attend_back/pallas_call | solution.py:240
  272.9 3.2 convert_reduce_fusion.1
  276.6 4.0 convolution_convert_fusion.5
  288.8 3.3 fusion.34
  295.1 4.1 add_convert_fusion
  299.2 4.5 %all-to-all-start.3 = ((bf16[8,1,128,768]{3,2,1,0:T(8,128)(2,1)}), bf16[8,1,128,768]{3,2,1,0:T(8,128)(2,1)}, u32[]{:S(2)}, u32[]{:S(2)}) async-start(bf16[8,1,128,768]{3,2,1,0:T(8,128)(2,1)} %bitcast.145), calls=%async_computation.3 | async-start | bytes 3145728 | tf_op jit(solution)/shard_map/all_to_all | solution.py:752
  304.6 3.4 pad_maximum_fusion.refs_0_
  308.0 9.9 %convolution_convert_fusion.1 = bf16[768,3072]{1,0:T(8,128)(2,1)} fusion(bf16[1024,3072]{1,0:T(8,128)(2,1)} %copy-done.25, f32[1024,768]{1,0:T(8,128)S(1)} %copy-done.1, f32[768]{0:T(1024)S(1)} %add.187, f32[768]{0:T(1024)S(1)} %mul.227, f32[1024]{0:T(1024)S(1)} %add_rsqrt_fusion.1, f32[1024]{0:T(1024)S(1)} %broadcast_multiply_fusion.4), kind=kOutput, calls=%fused_computation.29 | convolution fusion | flops 4838129664 | bytes 14170112 | tf_op jit(solution)/shard_map/dot_general | solution.py:29
  317.9 6.9 %all-to-all-done.3 = bf16[8,1,128,768]{3,2,1,0:T(8,128)(2,1)} async-done(((bf16[8,1,128,768]{3,2,1,0:T(8,128)(2,1)}), bf16[8,1,128,768]{3,2,1,0:T(8,128)(2,1)}, u32[]{:S(2)}, u32[]{:S(2)}) %all-to-all-start.3) | async-done | bytes 1572896 | tf_op jit(solution)/shard_map/all_to_all | solution.py:752
  324.8 3.6 all-to-all-start.1
  328.4 9.8 %convolution_convert_fusion = bf16[768,3072]{1,0:T(8,128)(2,1)} fusion(bf16[1024,3072]{1,0:T(8,128)(2,1)} %copy-done.26, f32[1024,768]{1,0:T(8,128)} %copy-done.7), kind=kOutput, calls=%fused_computation.28 | convolution fusion | flops 4834983936 | bytes 14155776 | tf_op jit(solution)/shard_map/dot_general | solution.py:29
  338.2 69.1 %scatter_grads.1 = (f32[3,48,384]{2,1,0:T(8,128)}, f32[48,1536]{1,0:T(8,128)}, f32[48,1536]{1,0:T(8,128)}, f32[48,384]{1,0:T(8,128)}, f32[16,128]{1,0:T(8,128)}) custom-call(bf16[3,16,48,768]{3,2,1,0:T(8,128)(2,1)} %pad_maximum_fusion.refs_0_, bf16[16,48,3072]{2,1,0:T(8,128)(2,1)} %bitcast.146, bf16[16,48,3072]{2,1,0:T(8,128)(2,1)} %bitcast.147, ...), custom_call_target="tpu_custom_call" | custom-call | tf_op jit(solution)/shard_map/scatter_grads/pallas_call | solution.py:652
  (138 shorter events, 41.2 us)
Async XLA Ops:
  0.6 5.4 %copy-start.24 = (bf16[192]{0:T(256)(128)(2,1)S(1)}, bf16[192]{0:T(256)(128)(2,1)}, u32[]{:S(2)}) copy-start(bf16[192]{0:T(256)(128)(2,1)} %param.23) | copy-start | bytes 1156
  0.7 5.5 %copy-start.16 = (bf16[48]{0:T(256)(128)(2,1)S(1)}, bf16[48]{0:T(256)(128)(2,1)}, u32[]{:S(2)}) copy-start(bf16[48]{0:T(256)(128)(2,1)} %param.22) | copy-start | bytes 292
  0.7 5.5 %copy-start.17 = (bf16[48]{0:T(256)(128)(2,1)S(1)}, bf16[48]{0:T(256)(128)(2,1)}, u32[]{:S(2)}) copy-start(bf16[48]{0:T(256)(128)(2,1)} %param.24) | copy-start | bytes 292
  0.7 5.5 %copy-start.18 = (bf16[48]{0:T(256)(128)(2,1)S(1)}, bf16[48]{0:T(256)(128)(2,1)}, u32[]{:S(2)}) copy-start(bf16[48]{0:T(256)(128)(2,1)} %param.25) | copy-start | bytes 292
  0.7 5.5 %copy-start.19 = (bf16[48]{0:T(256)(128)(2,1)S(1)}, bf16[48]{0:T(256)(128)(2,1)}, u32[]{:S(2)}) copy-start(bf16[48]{0:T(256)(128)(2,1)} %param.26) | copy-start | bytes 292
  0.7 5.5 %copy-start.20 = (bf16[48]{0:T(256)(128)(2,1)S(1)}, bf16[48]{0:T(256)(128)(2,1)}, u32[]{:S(2)}) copy-start(bf16[48]{0:T(256)(128)(2,1)} %param.27) | copy-start | bytes 292
  0.7 5.5 %copy-start.21 = (bf16[48]{0:T(256)(128)(2,1)S(1)}, bf16[48]{0:T(256)(128)(2,1)}, u32[]{:S(2)}) copy-start(bf16[48]{0:T(256)(128)(2,1)} %param.28) | copy-start | bytes 292
  0.7 5.5 %copy-start.15 = (bf16[3,48]{1,0:T(4,128)(2,1)S(1)}, bf16[3,48]{1,0:T(4,128)(2,1)}, u32[]{:S(2)}) copy-start(bf16[3,48]{1,0:T(4,128)(2,1)} %param.21) | copy-start | bytes 868
  0.7 101.8 %all-to-all-start = ((bf16[8,1,128,768]{3,2,1,0:T(8,128)(2,1)}), bf16[8,1,128,768]{3,2,1,0:T(8,128)(2,1)S(1)}, u32[]{:S(2)}, u32[]{:S(2)}) async-start(bf16[8,1,128,768]{3,2,1,0:T(8,128)(2,1)} %bitcast.150), calls=%async_computation | async-start | bytes 3145728 | tf_op jit(solution)/shard_map/all_to_all | solution.py:747
  102.6 95.2 %all-to-all-start.2 = ((bf16[8,1,128,768]{3,2,1,0:T(8,128)(2,1)}), bf16[8,1,128,768]{3,2,1,0:T(8,128)(2,1)}, u32[]{:S(2)}, u32[]{:S(2)}) async-start(bf16[8,1,128,768]{3,2,1,0:T(8,128)(2,1)} %bitcast.28), calls=%async_computation.2 | async-start | bytes 3145728 | tf_op jit(solution)/shard_map/all_to_all | solution.py:747
  106.9 46.0 %copy-start.22 = (bf16[16,48,768]{2,1,0:T(8,128)(2,1)S(1)}, bf16[16,48,768]{2,1,0:T(8,128)(2,1)}, u32[]{:S(2)}) copy-start(bf16[16,48,768]{2,1,0:T(8,128)(2,1)} %get-tuple-element.32) | copy-start | bytes 3538948
  152.9 38.8 %slice-start.4 = ((s8[4718592]{0:T(1024)(128)(4,1)}), s8[4194304]{0:T(1024)(128)(4,1)S(1)}, s32[]{:S(2)}) async-start(s8[4718592]{0:T(1024)(128)(4,1)} %bitcast.184), calls=%async_computation.8 | async-start | bytes 8388608
  156.5 35.2 %copy-start = (f32[1024,768]{1,0:T(8,128)}, f32[1024,768]{1,0:T(8,128)S(1)}, u32[]{:S(2)}) copy-start(f32[1024,768]{1,0:T(8,128)S(1)} %get-tuple-element.83) | copy-start | bytes 9437188
  157.1 34.7 %slice-start.5 = ((s8[4718592]{0:T(1024)(128)(4,1)}), s8[524288]{0:T(1024)(128)(4,1)S(1)}, s32[]{:S(2)}) async-start(s8[4718592]{0:T(1024)(128)(4,1)} %bitcast.184), calls=%async_computation.9 | async-start | bytes 1048576
  191.7 5.5 %copy-start.26 = (bf16[1024,3072]{1,0:T(8,128)(2,1)}, bf16[1024,3072]{1,0:T(8,128)(2,1)S(1)}, u32[]{:S(2)}) copy-start(bf16[1024,3072]{1,0:T(8,128)(2,1)S(1)} %get-tuple-element.84) | copy-start | bytes 18874372
  202.5 17.0 %slice-start.2 = ((s8[4718592]{0:T(1024)(128)(4,1)}), s8[4194304]{0:T(1024)(128)(4,1)S(1)}, s32[]{:S(2)}) async-start(s8[4718592]{0:T(1024)(128)(4,1)} %bitcast.180), calls=%async_computation.6 | async-start | bytes 8388608
  206.1 13.4 %copy-start.7 = (f32[1024,768]{1,0:T(8,128)}, f32[1024,768]{1,0:T(8,128)S(1)}, u32[]{:S(2)}) copy-start(f32[1024,768]{1,0:T(8,128)S(1)} %get-tuple-element.63) | copy-start | bytes 9437188
  206.1 13.5 %copy-start.1 = (f32[1024,768]{1,0:T(8,128)S(1)}, f32[1024,768]{1,0:T(8,128)}, u32[]{:S(2)}) copy-start(f32[1024,768]{1,0:T(8,128)} %copy-done) | copy-start | bytes 9437188
  206.1 13.5 %slice-start.3 = ((s8[4718592]{0:T(1024)(128)(4,1)}), s8[524288]{0:T(1024)(128)(4,1)S(1)}, s32[]{:S(2)}) async-start(s8[4718592]{0:T(1024)(128)(4,1)} %bitcast.180), calls=%async_computation.7 | async-start | bytes 1048576
  219.5 6.1 %copy-start.25 = (bf16[1024,3072]{1,0:T(8,128)(2,1)}, bf16[1024,3072]{1,0:T(8,128)(2,1)S(1)}, u32[]{:S(2)}) copy-start(bf16[1024,3072]{1,0:T(8,128)(2,1)S(1)} %get-tuple-element.90) | copy-start | bytes 18874372
  299.2 25.6 %all-to-all-start.3 = ((bf16[8,1,128,768]{3,2,1,0:T(8,128)(2,1)}), bf16[8,1,128,768]{3,2,1,0:T(8,128)(2,1)}, u32[]{:S(2)}, u32[]{:S(2)}) async-start(bf16[8,1,128,768]{3,2,1,0:T(8,128)(2,1)} %bitcast.145), calls=%async_computation.3 | async-start | bytes 3145728 | tf_op jit(solution)/shard_map/all_to_all | solution.py:752
  324.8 86.5 %all-to-all-start.1 = ((bf16[8,1,128,768]{3,2,1,0:T(8,128)(2,1)}), bf16[8,1,128,768]{3,2,1,0:T(8,128)(2,1)S(1)}, u32[]{:S(2)}, u32[]{:S(2)}) async-start(bf16[8,1,128,768]{3,2,1,0:T(8,128)(2,1)} %bitcast.143), calls=%async_computation.1 | async-start | bytes 3145728 | tf_op jit(solution)/shard_map/all_to_all | solution.py:752
  411.3 5.1 %copy-start.12 = (f32[48,1536]{1,0:T(8,128)S(1)}, f32[48,1536]{1,0:T(8,128)}, u32[]{:S(2)}) copy-start(f32[48,1536]{1,0:T(8,128)} %get-tuple-element.111) | copy-start | bytes 884740
  411.3 5.8 %copy-start.11 = (f32[48,1536]{1,0:T(8,128)S(1)}, f32[48,1536]{1,0:T(8,128)}, u32[]{:S(2)}) copy-start(f32[48,1536]{1,0:T(8,128)} %get-tuple-element.42) | copy-start | bytes 884740
  (14 other events, 47.0 us)

commit v3 on v2

--- a/solution.py
+++ b/solution.py
@@ -283,6 +283,255 @@
     rate = jnp.exp(column.astype(jnp.float32) * (-2.0 * math.log(10000.0) / HEAD_DIM))
     phase = position[:, None] * rate[None, :]
     return jnp.cos(phase), jnp.sin(phase)
+
+
+CHUNK = 512
+STEP = 16
+UNROLL = 4
+ATTEND_BIAS, DOWN_BIAS, FIRST_GAIN, FIRST_SHIFT, SECOND_GAIN, SECOND_SHIFT = range(3, 9)
+SUMS = 6
+
+
+def row_mean(values):
+    return jnp.sum(values, axis=-1, keepdims=True) * (1.0 / D)
+
+
+def fold(values):
+    return jnp.sum(values.reshape(values.shape[0] // 8, 8, values.shape[1]), axis=0)
+
+
+def chunk_at(index):
+    return pl.ds(pl.multiple_of(index * CHUNK, CHUNK), CHUNK)
+
+
+def ffn_kernel(
+    a_ref, attend_ref, wide_ref, shift_ref, x_hbm, c_hbm, up_hbm, down_hbm,
+    joined_ref, branch_ref, sums_ref, up_sums_ref, out_hbm, up_grad_hbm, down_grad_hbm, attend_grad_hbm,
+    x_ref, c_ref, up_ref, down_ref, out_ref, hidden_ref, slope_ref, low_ref, ffn_ref, turned_ref,
+    left, right, near, far, first, unit, acc, factor, sums, up_sums, stage, in_sem, out_sem, stage_sem,
+):
+    loads = [
+        pltpu.make_async_copy(source, target, in_sem.at[i])
+        for i, (source, target) in enumerate(
+            ((x_hbm, x_ref), (up_hbm, up_ref), (down_hbm, down_ref), (c_hbm, c_ref))
+        )
+    ]
+    for load in loads:
+        load.start()
+    sums[...] = jnp.zeros_like(sums)
+    up_sums[...] = jnp.zeros_like(up_sums)
+    pairs = FF // CHUNK // 2
+
+    def vector(index):
+        return wide_ref[pl.ds(index, 1), :]
+
+    def add_sum(index, values):
+        sums[index - ATTEND_BIAS] += fold(values)
+
+    def rows_loop(body):
+        @pl.loop(0, S // STEP, unroll=UNROLL)
+        def _(step):
+            body(pl.ds(pl.multiple_of(step * STEP, STEP), STEP))
+
+    acc[...] = dot(a_ref[...], attend_ref[...], NT)
+    loads[0].wait()
+
+    @rows_loop
+    def _(rows):
+        joined = x_ref[rows, :].astype(jnp.float32) + acc[rows, :] + vector(ATTEND_BIAS)
+        centred = joined - row_mean(joined)
+        scale = lax.rsqrt(row_mean(centred * centred) + norm_eps)
+        normed = centred * scale
+        unit[rows, :] = normed
+        factor[rows, :] = scale
+        result = normed * vector(FIRST_GAIN) + vector(FIRST_SHIFT)
+        first[rows, :] = result
+        low_ref[rows, :] = result.astype(jnp.bfloat16)
+
+    loads[1].wait()
+    loads[2].wait()
+
+    def expand(target, index):
+        target[...] = dot(low_ref[...], up_ref[:, chunk_at(index)], NN)
+
+    def activate(source, target, index):
+        pre = source[...] + shift_ref[:, chunk_at(index)]
+        cumulative = 0.5 + 0.5 * lax.erf(pre * (1.0 / math.sqrt(2.0)))
+        density = jnp.exp(-0.5 * pre * pre) * (1.0 / math.sqrt(2.0 * math.pi))
+        hidden = (pre * cumulative).astype(jnp.bfloat16)
+        target[...] = hidden
+        hidden_ref[:, chunk_at(index)] = hidden
+        slope_ref[:, chunk_at(index)] = (cumulative + pre * density).astype(jnp.bfloat16)
+
+    def contract(source, index):
+        acc[...] += dot(source[...], down_ref[:, chunk_at(index)], NT)
+
+    def forward(pair, last):
+        expand(right, 2 * pair + 1)
+        activate(left, near, 2 * pair)
+        if not last:
+            expand(left, 2 * pair + 2)
+        contract(near, 2 * pair)
+        activate(right, far, 2 * pair + 1)
+        contract(far, 2 * pair + 1)
+
+    expand(left, 0)
+    acc[...] = jnp.zeros_like(acc)
+
+    @pl.loop(0, pairs - 1)
+    def _(pair):
+        forward(pair, False)
+
+    forward(pairs - 1, True)
+    loads[3].wait()
+
+    @rows_loop
+    def _(rows):
+        joined = first[rows, :] + acc[rows, :] + vector(DOWN_BIAS)
+        centred = joined - row_mean(joined)
+        scale = lax.rsqrt(row_mean(centred * centred) + norm_eps)
+        normed = centred * scale
+        out_ref[rows, :] = (normed * vector(SECOND_GAIN) + vector(SECOND_SHIFT)).astype(jnp.bfloat16)
+        grad = c_ref[rows, :].astype(jnp.float32)
+        add_sum(SECOND_GAIN, grad * normed)
+        add_sum(SECOND_SHIFT, grad)
+        inner = grad * vector(SECOND_GAIN)
+        back = scale * (inner - row_mean(inner) - normed * row_mean(inner * normed))
+        first[rows, :] = back
+        low = back.astype(jnp.bfloat16)
+        ffn_ref[rows, :] = low
+        add_sum(DOWN_BIAS, low.astype(jnp.float32))
+
+    store = pltpu.make_async_copy(out_ref, out_hbm, out_sem)
+    store.start()
+
+    def stored(slot, target, index):
+        return pltpu.make_async_copy(
+            stage.at[slot], target.at[:, chunk_at(index)], stage_sem.at[slot]
+        )
+
+    def weight_grad(source, target):
+        @pl.loop(0, pairs)
+        def _(pair):
+            for slot in range(2):
+                index = 2 * pair + slot
+
+                @pl.when(pair > 0)
+                def _():
+                    stored(slot, target, index).wait()
+
+                stage[slot] = dot(turned_ref[...], source[:, chunk_at(index)], NN).astype(jnp.bfloat16)
+                stored(slot, target, index).start()
+
+        for slot in range(2):
+            stored(slot, target, slot).wait()
+
+    turned_ref[...] = jnp.transpose(ffn_ref[...])
+    weight_grad(hidden_ref, down_grad_hbm)
+
+    def widen(target, index):
+        target[...] = dot(ffn_ref[...], down_ref[:, chunk_at(index)], NN)
+
+    def reweigh(source, target, index):
+        grad = (source[...] * slope_ref[:, chunk_at(index)].astype(jnp.float32)).astype(jnp.bfloat16)
+        target[...] = grad
+        hidden_ref[:, chunk_at(index)] = grad
+        up_sums[:, chunk_at(index)] += fold(grad.astype(jnp.float32))
+
+    def collect(source, index):
+        acc[...] += dot(source[...], up_ref[:, chunk_at(index)], NT)
+
+    def backward(pair, last):
+        widen(right, 2 * pair + 1)
+        reweigh(left, near, 2 * pair)
+        if not last:
+            widen(left, 2 * pair + 2)
+        collect(near, 2 * pair)
+        reweigh(right, far, 2 * pair + 1)
+        collect(far, 2 * pair + 1)
+
+    widen(left, 0)
+    acc[...] = jnp.zeros_like(acc)
+
+    @pl.loop(0, pairs - 1)
+    def _(pair):
+        backward(pair, False)
+
+    backward(pairs - 1, True)
+
+    @rows_loop
+    def _(rows):
+        grad = first[rows, :] + acc[rows, :]
+        normed = unit[rows, :]
+        add_sum(FIRST_GAIN, grad * normed)
+        add_sum(FIRST_SHIFT, grad)
+        inner = grad * vector(FIRST_GAIN)
+        back = factor[rows, :] * (inner - row_mean(inner) - normed * row_mean(inner * normed))
+        low = back.astype(jnp.bfloat16)
+        branch_ref[rows, :] = low
+        add_sum(ATTEND_BIAS, low.astype(jnp.float32))
+
+    joined_ref[...] = dot(branch_ref[...], attend_ref[...], NN).astype(jnp.bfloat16)
+    turned_ref[...] = jnp.transpose(low_ref[...])
+    weight_grad(hidden_ref, up_grad_hbm)
+    turned_ref[...] = jnp.transpose(branch_ref[...])
+    half = D // 2
+    for slot in range(2):
+        part = stage.at[slot, :, :half]
+        stage[slot, :, :half] = dot(
+            turned_ref[...], a_ref[:, slot * half : (slot + 1) * half], NN
+        ).astype(jnp.bfloat16)
+        pltpu.make_async_copy(
+            part, attend_grad_hbm.at[:, slot * half : (slot + 1) * half], stage_sem.at[slot]
+        ).start()
+    for index in range(SUMS):
+        sums_ref[pl.ds(index, 1), :] = jnp.sum(sums[index], axis=0, keepdims=True)
+    up_sums_ref[...] = jnp.sum(up_sums[...], axis=0, keepdims=True)
+    for slot in range(2):
+        pltpu.make_async_copy(
+            stage.at[slot, :, :half],
+            attend_grad_hbm.at[:, slot * half : (slot + 1) * half],
+            stage_sem.at[slot],
+        ).wait()
+    store.wait()
+
+
+def feed_forward(attended, x, cotangent, attend_t, up, down_t, wide, up_shift):
+    vmem, hbm = pl.BlockSpec(memory_space=pltpu.VMEM), pl.BlockSpec(memory_space=pl.ANY)
+
+    def low(*shape):
+        return jax.ShapeDtypeStruct(shape, jnp.bfloat16)
+
+    def full(*shape):
+        return jax.ShapeDtypeStruct(shape, jnp.float32)
+
+    def scratch(width, kind=jnp.bfloat16):
+        return pltpu.VMEM((S, width), kind)
+
+    return pl.pallas_call(
+        ffn_kernel,
+        in_specs=[vmem] * 4 + [hbm] * 4,
+        out_specs=[vmem] * 4 + [hbm] * 4,
+        out_shape=[
+            low(S, D), low(S, D), full(SUMS, D), full(1, FF), low(S, D), low(D, FF), low(D, FF),
+            low(D, D),
+        ],
+        scratch_shapes=[
+            scratch(D), scratch(D), pltpu.VMEM((D, FF), jnp.bfloat16), pltpu.VMEM((D, FF), jnp.bfloat16),
+            scratch(D), scratch(FF), scratch(FF), scratch(D), scratch(D), pltpu.VMEM((D, S), jnp.bfloat16),
+            scratch(CHUNK, jnp.float32), scratch(CHUNK, jnp.float32), scratch(CHUNK), scratch(CHUNK),
+            scratch(D, jnp.float32), scratch(D, jnp.float32), scratch(D, jnp.float32),
+            scratch(1, jnp.float32),
+            pltpu.VMEM((SUMS, 8, D), jnp.float32), pltpu.VMEM((8, FF), jnp.float32),
+            pltpu.VMEM((2, D, CHUNK), jnp.bfloat16),
+            pltpu.SemaphoreType.DMA((4,)), pltpu.SemaphoreType.DMA, pltpu.SemaphoreType.DMA((2,)),
+        ],
+        compiler_params=pltpu.CompilerParams(vmem_limit_bytes=63 << 20),
+        name="feed_forward",
+        cost_estimate=pl.CostEstimate(
+            flops=6 * S * D * (D + 2 * FF), bytes_accessed=30 << 20, transcendentals=2 * S * FF
+        ),
+    )(attended, attend_t, wide, up_shift.reshape(1, FF), x, cotangent, up, down_t)
 
 
 MESH = pl.DeviceIdType.MESH
@@ -674,32 +923,6 @@
     return dict(zip(ITEMS, outs))
 
 
-def normalize(rows, gain, shift):
-    mean = jnp.mean(rows, axis=-1, keepdims=True)
-    centred = rows - mean
-    factor = lax.rsqrt(jnp.mean(centred * centred, axis=-1, keepdims=True) + norm_eps)
-    unit = centred * factor
-    return (unit * gain + shift, unit, factor)
-
-
-def normalize_back(incoming, unit, factor, gain):
-    gain_grad = jnp.sum(incoming * unit, axis=0)
-    shift_grad = jnp.sum(incoming, axis=0)
-    inner = incoming * gain
-    rows_grad = factor * (
-        inner
-        - jnp.mean(inner, axis=-1, keepdims=True)
-        - unit * jnp.mean(inner * unit, axis=-1, keepdims=True)
-    )
-    return (rows_grad, gain_grad, shift_grad)
-
-
-def gelu_slope(values):
-    cumulative = 0.5 * (1.0 + lax.erf(values * (1.0 / math.sqrt(2.0))))
-    density = jnp.exp(-0.5 * values * values) * (1.0 / math.sqrt(2.0 * math.pi))
-    return cumulative + values * density
-
-
 def fitting(shards):
     return lax.axis_size("ctx") == 4 and lax.axis_size("tp") == 2 and shards["up"].shape[0] % 16 == 0
 
@@ -790,38 +1013,24 @@
     query, key, value, attended, level = attend(
         tables[0], tables[1], x, project, wide[:3], cosine, sine, *tables[2:]
     )
+    incoming = to_sequences(cotangent)
+    parts = [
+        feed_forward(attended[i], x[i], incoming[i], attend_t, up, down_t, wide, up_shift)
+        for i in range(own)
+    ]
+    attended_grad = jnp.stack([part[0] for part in parts])
+    branch_grad = jnp.concatenate([part[1] for part in parts])
+    sums = sum(part[2] for part in parts)
+    up_bias_grad = sum(part[3] for part in parts)
+    output = to_blocks(jnp.stack([part[4] for part in parts]))
+    up_grad, down_grad, attend_grad = (
+        parts[0][k] if own == 1 else sum(part[k].astype(jnp.float32) for part in parts).astype(jnp.bfloat16)
+        for k in (5, 6, 7)
+    )
     flat = x.reshape(rows, D)
-    attended_flat = attended.reshape(rows, D)
-    branch = dot(attended_flat, attend_t, NT) + wide[3]
-    first, first_unit, first_factor = normalize(flat.astype(jnp.float32) + branch, wide[5], wide[6])
-    first_low = first.astype(jnp.bfloat16)
-    pre = dot(first_low, up, NN) + up_shift
-    hidden = jax.nn.gelu(pre, approximate=False).astype(jnp.bfloat16)
-    ffn = dot(hidden, down_t, NT) + wide[4]
-    second, second_unit, second_factor = normalize(first + ffn, wide[7], wide[8])
-    output = to_blocks(second.astype(jnp.bfloat16).reshape(own, S, D))
-
-    incoming = to_sequences(cotangent).reshape(rows, D).astype(jnp.float32)
-    second_grad, second_gain_grad, second_shift_grad = normalize_back(
-        incoming, second_unit, second_factor, wide[7]
-    )
-    ffn_grad = second_grad.astype(jnp.bfloat16)
-    down_bias_grad = jnp.sum(ffn_grad.astype(jnp.float32), axis=0)
-    down_t_grad = dot(ffn_grad, hidden, TN)
-    pre_grad = (dot(ffn_grad, down_t, NN) * gelu_slope(pre)).astype(jnp.bfloat16)
-    up_bias_grad = jnp.sum(pre_grad.astype(jnp.float32), axis=0)
-    up_grad = dot(first_low, pre_grad, TN)
-    first_total = second_grad + dot(pre_grad, up, NT)
-    first_grad, first_gain_grad, first_shift_grad = normalize_back(
-        first_total, first_unit, first_factor, wide[5]
-    )
-    branch_grad = first_grad.astype(jnp.bfloat16)
-    attend_bias_grad = jnp.sum(branch_grad.astype(jnp.float32), axis=0)
-    attend_t_grad = dot(branch_grad, attended_flat, TN)
-    attended_grad = dot(branch_grad, attend_t, NN).astype(jnp.bfloat16)
 
     joint_grad = attend_back(
-        tables[0], tables[1], query, key, value, attended, attended_grad.reshape(own, S, D), level,
+        tables[0], tables[1], query, key, value, attended, attended_grad, level,
         cosine, sine, *tables[2:],
     ).reshape(rows, 3 * D)
     project_bias_grad = jnp.sum(joint_grad.astype(jnp.float32), axis=0).reshape(3, D)
@@ -831,20 +1040,9 @@
     token_part = sum(
         dot(joint_grad[:, i * D : (i + 1) * D], project[i], NT) for i in range(3)
     )
-    tokens_grad = to_blocks((first_grad + token_part).astype(jnp.bfloat16).reshape(own, S, D))
-
-    sums = jnp.concatenate(
-        [
-            project_bias_grad,
-            attend_bias_grad[None],
-            down_bias_grad[None],
-            first_gain_grad[None],
-            first_shift_grad[None],
-            second_gain_grad[None],
-            second_shift_grad[None],
-        ],
-        axis=0,
-    )
+    tokens_grad = to_blocks((branch_grad.astype(jnp.float32) + token_part).astype(jnp.bfloat16).reshape(own, S, D))
+
+    sums = jnp.concatenate([project_bias_grad, sums], axis=0)
     sums = jnp.concatenate(
         [
             jnp.transpose(sums.reshape(9, pieces, depth), (1, 0, 2)),
@@ -854,9 +1052,9 @@
     )
     grads = {
         "project": project_grad.astype(jnp.bfloat16).reshape(3, pieces, depth, D),
-        "up": up_grad.astype(jnp.bfloat16).reshape(pieces, depth, FF),
-        "down": down_t_grad.astype(jnp.bfloat16).reshape(pieces, depth, FF),
-        "attend": attend_t_grad.astype(jnp.bfloat16).reshape(pieces, depth, D),
+        "up": up_grad.reshape(pieces, depth, FF),
+        "down": down_grad.reshape(pieces, depth, FF),
+        "attend": attend_grad.reshape(pieces, depth, D),
         "vectors": jnp.pad(sums, ((0, 0), (0, 3), (0, LANES - depth))),
     }
     shards = scatter_grads(grads) if custom else scatter_plain(grads)

time: 426 us -> 398 us (0.934)
  matrix products: 107 us -> 17.5 us
  Pallas kernels: 240 us -> 311 us
  other arithmetic: 25.9 us -> 14.8 us
  waiting for transfers between devices: 6.92 us -> 13.7 us
    dot_general x15 -> x6, matrix products: 107 us -> 17.5 us  [dot(): lax.dot_general(left, right, dims, preferred_element_type=jnp.float32)]
    pallas_call x0 -> x1, Pallas kernels: none -> 71.9 us  [feed_forward(): pl.pallas_call(ffn_kernel, in_specs=[vmem] * 4 + [hbm] * 4, out_specs=[vm...]
    reduce_sum x6 -> x0, other arithmetic: 10.4 us -> none  [the longest x1 3.56 us: local(): down_bias_grad = jnp.sum(ffn_grad.astype(jnp.float32), axis=0)]
    all_to_all x2, waiting for transfers between devices: 6.91 us -> 13.7 us  [to_blocks(): return lax.all_to_all(parts, SEQ, 0, 0, tiled=True).reshape(tokens.shape)]
  transfers between devices with their start and end apart: 4 -> 4, of which waited for: 1 -> 1; matrix products, arithmetic and copies ran while one was open for 21% -> 9% of each run, Pallas kernels for 47% -> 50%
where the time goes in v3:
time: 398 us; the launch traced here: 394 us
  Pallas kernels  311 us (78%)
  starting transfers between devices  18.2 us (5%)
  local copies, waits for them, and re-layouts  17.5 us (4%)
  matrix products  17.5 us (4%)
  other arithmetic  14.8 us (4%)
  waiting for transfers between devices  13.7 us (3%)
    pallas_call x1, Pallas kernels, gather_weights(): pl.pallas_call(lambda *refs: gather_kernel(widths, chips, *refs), out_sha...  81 us
    pallas_call x1, Pallas kernels, feed_forward(): pl.pallas_call(ffn_kernel, in_specs=[vmem] * 4 + [hbm] * 4, out_specs=[vm...  71.9 us
    pallas_call x1, Pallas kernels, scatter_grads(): pl.pallas_call(lambda *refs: scatter_kernel(widths, chips, *refs), out_sh...  68.9 us
    pallas_call x1, Pallas kernels, attend(): pl.pallas_call(attend_kernel, grid_spec=pltpu.PrefetchScalarGridSpec(num_...  45.9 us
    pallas_call x1, Pallas kernels, attend_back(): pl.pallas_call(attend_back_kernel, grid_spec=pltpu.PrefetchScalarGridSpec...  43.4 us
    dot_general x6, matrix products, dot(): lax.dot_general(left, right, dims, preferred_element_type=jnp.float32)  17.5 us
    all_to_all x2, waiting for transfers between devices, to_blocks(): return lax.all_to_all(parts, SEQ, 0, 0, tiled=True).reshape(tokens.shape)  13.7 us
    all_to_all x2, starting transfers between devices, to_sequences(): parts = lax.all_to_all(parts, SEQ, 0, 0, tiled=True)  10.1 us
  transfers between devices with their start and end apart: 4, of which 1 were waited for; matrix products, arithmetic and copies ran while one was open for 9% of the time, Pallas kernels for 50%

profile of v3, /device:TPU:0, one launch (start us, length us, event | category | flops | bytes accessed | tf_op | source)
XLA Modules:
  0.0 394.0 jit_solution(9832285491845674117)
XLA Ops:
  0.7 5.3 %all-to-all-start = ((bf16[8,1,128,768]{3,2,1,0:T(8,128)(2,1)}), bf16[8,1,128,768]{3,2,1,0:T(8,128)(2,1)S(1)}, u32[]{:S(2)}, u32[]{:S(2)}) async-start(bf16[8,1,128,768]{3,2,1,0:T(8,128)(2,1)} %bitcast.114), calls=%async_computation | async-start | bytes 3145728 | tf_op jit(solution)/shard_map/all_to_all | solution.py:970
  6.9 81.0 %gather_weights.1 = (bf16[3,16,48,768]{3,2,1,0:T(8,128)(2,1)}, bf16[16,48,3072]{2,1,0:T(8,128)(2,1)}, bf16[16,48,3072]{2,1,0:T(8,128)(2,1)}, bf16[16,48,768]{2,1,0:T(8,128)(2,1)}, bf16[16,16,128]{2,1,0:T(8,128)(2,1)}) custom-call(bf16[3,48,384]{2,1,0:T(8,128)(2,1)} %bitcast.133, bf16[48,1536]{1,0:T(8,128)(2,1)} %refs_1_.1, bf16[48,1536]{1,0:T(8,128)(2,1)} %bitcast.130, ...), custom_call_target="tpu_custom_call" | custom-call | tf_op jit(solution)/shard_map/gather_weights/pallas_call | solution.py:748
  88.9 1.4 add_bitcast_fusion
  94.6 1.4 fusion.17.low_ref
  97.1 4.8 %all-to-all-start.1 = ((bf16[8,1,128,768]{3,2,1,0:T(8,128)(2,1)}), bf16[8,1,128,768]{3,2,1,0:T(8,128)(2,1)}, u32[]{:S(2)}, u32[]{:S(2)}) async-start(bf16[8,1,128,768]{3,2,1,0:T(8,128)(2,1)} %bitcast.115), calls=%async_computation.1 | async-start | bytes 3145728 | tf_op jit(solution)/shard_map/all_to_all | solution.py:970
  102.4 3.0 multiply_sine_fusion
  105.4 1.9 fusion.10
  107.3 45.9 %attend.1 = (bf16[1,1024,768]{2,1,0:T(8,128)(2,1)}, bf16[1,1024,768]{2,1,0:T(8,128)(2,1)}, bf16[1,1024,768]{2,1,0:T(8,128)(2,1)}, bf16[1,1024,768]{2,1,0:T(8,128)(2,1)}, f32[1,12,1024]{2,1,0:T(8,128)}) custom-call(s32[1,8]{1,0:T(1,128)} %get-tuple-element.78.first_ref, s32[1,8]{1,0:T(1,128)} %get-tuple-element.77.count_ref, bf16[1,1024,768]{2,1,0:T(8,128)(2,1)} %bitcast.116, ...), custom_call_target="tpu_custom_call" | custom-call | flops 6000000000 | bytes 12582912 | tf_op jit(solution)/shard_map/attend/pallas_call | solution.py:214
  153.2 71.9 %feed_forward.1 = (bf16[1024,768]{1,0:T(8,128)(2,1)}, bf16[1024,768]{1,0:T(8,128)(2,1)}, f32[6,768]{1,0:T(8,128)}, f32[1,3072]{1,0:T(1,128)}, bf16[1024,768]{1,0...) custom-call(bf16[1024,768]{1,0:T(8,128)(2,1)} %bitcast.145, ...), custom_call_target="tpu_custom_call" | custom-call | flops 32614907904 | bytes 31457280 | tf_op jit(solution)/shard_map/feed_forward/pallas_call | solution.py:511
  225.0 43.4 %attend_back.1 = bf16[1,1024,2304]{2,1,0:T(8,128)(2,1)} custom-call(s32[1,8]{1,0:T(1,128)} %get-tuple-element.78.first_ref, s32[1,8]{1,0:T(1,128)} %get-tuple-element.77.count_ref, bf16[1,1024,768]{2,1,0:T(8,128)(2,1)} %get-tuple-element.45.q_ref, bf16[1,1024,768]{2,1,0:T(8,128)(2,1)} %get-tuple-element.46.k_ref, ...), custom_call_target="tpu_custom_call" | custom-call | flops 12000000000 | bytes 14680064 | tf_op jit(solution)/shard_map/attend_back/pallas_call | solution.py:240
  268.5 3.0 fusion.3
  271.6 1.4 fusion.6
  273.4 2.8 add_convert_fusion
  276.2 4.5 %all-to-all-start.3 = ((bf16[8,1,128,768]{3,2,1,0:T(8,128)(2,1)}), bf16[8,1,128,768]{3,2,1,0:T(8,128)(2,1)S(1)}, u32[]{:S(2)}, u32[]{:S(2)}) async-start(bf16[8,1,128,768]{3,2,1,0:T(8,128)(2,1)} %bitcast.36), calls=%async_computation.3 | async-start | bytes 3145728 | tf_op jit(solution)/shard_map/all_to_all | solution.py:975
  280.7 3.2 convert_reduce_fusion
  284.0 3.9 convolution_convert_fusion.2
  287.9 13.7 %all-to-all-done.3 = bf16[8,1,128,768]{3,2,1,0:T(8,128)(2,1)S(1)} async-done(((bf16[8,1,128,768]{3,2,1,0:T(8,128)(2,1)}), bf16[8,1,128,768]{3,2,1,0:T(8,128)(2,1)S(1)}, u32[]{:S(2)}, u32[]{:S(2)}) %all-to-all-start.3) | async-done | bytes 1572896 | tf_op jit(solution)/shard_map/all_to_all | solution.py:975
  301.6 3.7 all-to-all-start.2
  307.4 3.4 convolution_convert_fusion.1
  310.8 3.0 convolution_convert_fusion
  313.8 2.1 pad_maximum_fusion.refs_0_
  315.9 68.9 %scatter_grads.1 = (f32[3,48,384]{2,1,0:T(8,128)}, f32[48,1536]{1,0:T(8,128)}, f32[48,1536]{1,0:T(8,128)}, f32[48,384]{1,0:T(8,128)}, f32[16,128]{1,0:T(8,128)}) custom-call(bf16[3,16,48,768]{3,2,1,0:T(8,128)(2,1)} %pad_maximum_fusion.refs_0_, bf16[16,48,3072]{2,1,0:T(8,128)(2,1)} %bitcast.111, bf16[16,48,3072]{2,1,0:T(8,128)(2,1)} %bitcast.112, ...), custom_call_target="tpu_custom_call" | custom-call | tf_op jit(solution)/shard_map/scatter_grads/pallas_call | solution.py:901
  385.5 1.3 slice.91
  387.4 1.4 slice_bitcast_fusion.1
  (87 shorter events, 16.8 us)
Async XLA Ops:
  0.6 5.4 %copy-start.23 = (bf16[192]{0:T(256)(128)(2,1)S(1)}, bf16[192]{0:T(256)(128)(2,1)}, u32[]{:S(2)}) copy-start(bf16[192]{0:T(256)(128)(2,1)} %param.23) | copy-start | bytes 1156
  0.7 5.5 %copy-start.16 = (bf16[3,48]{1,0:T(4,128)(2,1)S(1)}, bf16[3,48]{1,0:T(4,128)(2,1)}, u32[]{:S(2)}) copy-start(bf16[3,48]{1,0:T(4,128)(2,1)} %param.21) | copy-start | bytes 868
  0.7 5.5 %copy-start.17 = (bf16[48]{0:T(256)(128)(2,1)S(1)}, bf16[48]{0:T(256)(128)(2,1)}, u32[]{:S(2)}) copy-start(bf16[48]{0:T(256)(128)(2,1)} %param.22) | copy-start | bytes 292
  0.7 5.5 %copy-start.18 = (bf16[48]{0:T(256)(128)(2,1)S(1)}, bf16[48]{0:T(256)(128)(2,1)}, u32[]{:S(2)}) copy-start(bf16[48]{0:T(256)(128)(2,1)} %param.24) | copy-start | bytes 292
  0.7 5.5 %copy-start.19 = (bf16[48]{0:T(256)(128)(2,1)S(1)}, bf16[48]{0:T(256)(128)(2,1)}, u32[]{:S(2)}) copy-start(bf16[48]{0:T(256)(128)(2,1)} %param.25) | copy-start | bytes 292
  0.7 5.5 %copy-start.20 = (bf16[48]{0:T(256)(128)(2,1)S(1)}, bf16[48]{0:T(256)(128)(2,1)}, u32[]{:S(2)}) copy-start(bf16[48]{0:T(256)(128)(2,1)} %param.26) | copy-start | bytes 292
  0.7 5.5 %copy-start.21 = (bf16[48]{0:T(256)(128)(2,1)S(1)}, bf16[48]{0:T(256)(128)(2,1)}, u32[]{:S(2)}) copy-start(bf16[48]{0:T(256)(128)(2,1)} %param.27) | copy-start | bytes 292
  0.7 5.5 %copy-start.22 = (bf16[48]{0:T(256)(128)(2,1)S(1)}, bf16[48]{0:T(256)(128)(2,1)}, u32[]{:S(2)}) copy-start(bf16[48]{0:T(256)(128)(2,1)} %param.28) | copy-start | bytes 292
  0.7 95.2 %all-to-all-start = ((bf16[8,1,128,768]{3,2,1,0:T(8,128)(2,1)}), bf16[8,1,128,768]{3,2,1,0:T(8,128)(2,1)S(1)}, u32[]{:S(2)}, u32[]{:S(2)}) async-start(bf16[8,1,128,768]{3,2,1,0:T(8,128)(2,1)} %bitcast.114), calls=%async_computation | async-start | bytes 3145728 | tf_op jit(solution)/shard_map/all_to_all | solution.py:970
  97.1 8.4 %copy-start.2 = (bf16[3,16,48,768]{3,2,1,0:T(8,128)(2,1)S(1)}, bf16[3,16,48,768]{3,2,1,0:T(8,128)(2,1)}, u32[]{:S(2)}) copy-start(bf16[3,16,48,768]{3,2,1,0:T(8,128)(2,1)} %get-tuple-element.37) | copy-start | bytes 10616836
  97.1 56.1 %all-to-all-start.1 = ((bf16[8,1,128,768]{3,2,1,0:T(8,128)(2,1)}), bf16[8,1,128,768]{3,2,1,0:T(8,128)(2,1)}, u32[]{:S(2)}, u32[]{:S(2)}) async-start(bf16[8,1,128,768]{3,2,1,0:T(8,128)(2,1)} %bitcast.115), calls=%async_computation.1 | async-start | bytes 3145728 | tf_op jit(solution)/shard_map/all_to_all | solution.py:970
  225.0 43.4 %copy-start.8 = (bf16[1,16,48,768]{3,2,1,0:T(8,128)(2,1)S(1)}, bf16[1,16,48,768]{3,2,1,0:T(8,128)(2,1)}, u32[]{:S(2)}) copy-start(bf16[1,16,48,768]{3,2,1,0:T(8,128)(2,1)} %get-tuple-element.67) | copy-start | bytes 3538948
  268.5 3.0 copy-start
  268.5 3.2 copy-start.7
  276.2 25.5 %all-to-all-start.3 = ((bf16[8,1,128,768]{3,2,1,0:T(8,128)(2,1)}), bf16[8,1,128,768]{3,2,1,0:T(8,128)(2,1)S(1)}, u32[]{:S(2)}, u32[]{:S(2)}) async-start(bf16[8,1,128,768]{3,2,1,0:T(8,128)(2,1)} %bitcast.36), calls=%async_computation.3 | async-start | bytes 3145728 | tf_op jit(solution)/shard_map/all_to_all | solution.py:975
  280.6 3.3 copy-start.14
  280.6 3.4 copy-start.5
  301.6 4.3 %copy-start.15 = (f32[1,3072]{1,0:T(1,128)S(1)}, f32[1,3072]{1,0:T(1,128)}, u32[]{:S(2)}) copy-start(f32[1,3072]{1,0:T(1,128)} %get-tuple-element.54) | copy-start | bytes 36868
  301.6 87.1 %all-to-all-start.2 = ((bf16[8,1,128,768]{3,2,1,0:T(8,128)(2,1)}), bf16[8,1,128,768]{3,2,1,0:T(8,128)(2,1)S(1)}, u32[]{:S(2)}, u32[]{:S(2)}) async-start(bf16[8,1,128,768]{3,2,1,0:T(8,128)(2,1)} %bitcast.121), calls=%async_computation.2 | async-start | bytes 3145728 | tf_op jit(solution)/shard_map/all_to_all | solution.py:975
  307.4 3.5 copy-start.6
  310.8 3.0 copy-start.9
  389.9 1.8 copy-start.13
  389.9 2.5 copy-start.11
  389.9 3.2 copy-start.10
  (4 other events, 5.5 us)
